TPU v7x, 512 devices: a whole 4x4x16 slice. The times are simulated.
512 devices in a mesh: gauss: 128 (over z, x, core), view: 4 (over y).
Axes of the slice: x: 4, y: 4, z: 16, core: 2. Of those that a mesh axis runs over, the one named last changes fastest.
Arguments:
- params: bfloat16 [64, 131072], P(None, 'gauss'), may hold values from -5 to 2, as said below
- lists: int32 [2048, 128], P(('gauss', 'view')), may hold values from -1 to 131071, as said below
- tile_pos: int32 [2048], P(('gauss', 'view')), may hold values from 0 to 255
- cam_index: int32 [2048], P(('gauss', 'view')), may hold values from 0 to 15
- cams: float32 [28, 16], replicated, may hold values from -1 to 1100, as said below
- targets: float32 [3, 2048, 256], P(None, ('gauss', 'view')), may hold values from 0 to 1
Outputs:
- rendered: float32 [3, 2048, 256], P(None, ('gauss', 'view'))
- grads: float32 [64, 131072], P(None, 'gauss')
Inputs may be any that keep to these rules, and one draw needn't show every extreme that they name: `lists`: within each tile the entries that are not -1 come first. The entries of one device's 4 tiles that are not -1 name at most 4 times Gaussians of one gauss index (blocks of 1024 consecutive Gaussians), and in every draw some gauss index is named exactly 4 times by the tiles of every device; the number of entries that are not -1 differs from device to device. `cams`: columns are cameras: rows 0-8 a rotation matrix, 9-11 a translation putting every Gaussian mean at depth 2.4 or more, row 12 the focal length, rows 13-27 appearance weights. `params`: rows 6-9 are quaternions whose first component is 1 or more.
All inputs are finite; a program needn't handle non-finite values.
Results may differ from a plain program's by a relative error of at most 0.0003.
Values may be sent and summed in bfloat16 or wider, within the bound.
A program may use at most 64 MiB of HBM per device.

v0:
```python
import jax
import jax.numpy as jnp
from jax import lax
from jax.sharding import PartitionSpec as P

WIN = 16


HIGH = lax.Precision.HIGHEST


def sh_terms(dir_x, dir_y, dir_z):
    return [
        jnp.ones_like(dir_x),
        dir_x,
        dir_y,
        dir_z,
        dir_x * dir_y,
        dir_y * dir_z,
        dir_x * dir_z,
        dir_x * dir_x - dir_y * dir_y,
        3.0 * dir_z * dir_z - 1.0,
        dir_x * (dir_x * dir_x - 3.0 * dir_y * dir_y),
        dir_x * dir_y * dir_z,
        dir_y * (3.0 * dir_x * dir_x - dir_y * dir_y),
        dir_z * (dir_x * dir_x - dir_y * dir_y),
        dir_x * (5.0 * dir_z * dir_z - 1.0),
        dir_y * (5.0 * dir_z * dir_z - 1.0),
        dir_z * (5.0 * dir_z * dir_z - 3.0),
    ]


def fix_rows(row_vals, is_live):
    return row_vals.at[6].set(jnp.where(is_live, row_vals[6], 1.0))


def project(row_vals, camcols):
    mean_x, mean_y, mean_z = (row_vals[0], row_vals[1], row_vals[2])
    cam_rot = [camcols[index] for index in range(9)]
    focal = camcols[12]
    cam_x = cam_rot[0] * mean_x + cam_rot[1] * mean_y + cam_rot[2] * mean_z + camcols[9]
    cam_y = cam_rot[3] * mean_x + cam_rot[4] * mean_y + cam_rot[5] * mean_z + camcols[10]
    cam_z = cam_rot[6] * mean_x + cam_rot[7] * mean_y + cam_rot[8] * mean_z + camcols[11]
    inv_z = 1.0 / cam_z
    quaternion = row_vals[6:10]
    q_norm = jnp.sqrt(jnp.sum(quaternion * quaternion, axis=0))
    unit_w = quaternion[0] / q_norm
    unit_x = quaternion[1] / q_norm
    unit_y = quaternion[2] / q_norm
    unit_z = quaternion[3] / q_norm
    rotation = [
        [
            1.0 - 2.0 * (unit_y * unit_y + unit_z * unit_z),
            2.0 * (unit_x * unit_y - unit_w * unit_z),
            2.0 * (unit_x * unit_z + unit_w * unit_y),
        ],
        [
            2.0 * (unit_x * unit_y + unit_w * unit_z),
            1.0 - 2.0 * (unit_x * unit_x + unit_z * unit_z),
            2.0 * (unit_y * unit_z - unit_w * unit_x),
        ],
        [
            2.0 * (unit_x * unit_z - unit_w * unit_y),
            2.0 * (unit_y * unit_z + unit_w * unit_x),
            1.0 - 2.0 * (unit_x * unit_x + unit_y * unit_y),
        ],
    ]
    mixed = [
        [
            cam_rot[3 * row_i] * rotation[0][col_k]
            + cam_rot[3 * row_i + 1] * rotation[1][col_k]
            + cam_rot[3 * row_i + 2] * rotation[2][col_k]
            for col_k in range(3)
        ]
        for row_i in range(3)
    ]
    jac_scale = focal * inv_z
    proj_u = [
        jac_scale * mixed[0][col_k] - jac_scale * cam_x * inv_z * mixed[2][col_k]
        for col_k in range(3)
    ]
    proj_v = [
        jac_scale * mixed[1][col_k] - jac_scale * cam_y * inv_z * mixed[2][col_k]
        for col_k in range(3)
    ]
    var_diag = jnp.exp(2.0 * row_vals[3:6])
    cov_a = (
        proj_u[0] * proj_u[0] * var_diag[0]
        + proj_u[1] * proj_u[1] * var_diag[1]
        + proj_u[2] * proj_u[2] * var_diag[2]
        + 0.3
    )
    cov_b = (
        proj_u[0] * proj_v[0] * var_diag[0]
        + proj_u[1] * proj_v[1] * var_diag[1]
        + proj_u[2] * proj_v[2] * var_diag[2]
    )
    cov_c = (
        proj_v[0] * proj_v[0] * var_diag[0]
        + proj_v[1] * proj_v[1] * var_diag[1]
        + proj_v[2] * proj_v[2] * var_diag[2]
        + 0.3
    )
    determinant = cov_a * cov_c - cov_b * cov_b
    opacity = jax.nn.sigmoid(row_vals[10])
    distance = jnp.sqrt(cam_x * cam_x + cam_y * cam_y + cam_z * cam_z)
    terms = sh_terms(cam_x / distance, cam_y / distance, cam_z / distance)
    colors = []
    for chan in range(3):
        shade = 0.5 + sum(
            (row_vals[11 + 16 * chan + basis_b] * terms[basis_b] for basis_b in range(16))
        )
        shade = shade + sum(
            (row_vals[59 + feat_j] * camcols[13 + 3 * feat_j + chan] for feat_j in range(5))
        )
        colors.append(shade)
    centre_u = focal * cam_x * inv_z
    centre_v = focal * cam_y * inv_z
    return jnp.stack(
        [
            centre_u,
            centre_v,
            cov_c / determinant,
            -cov_b / determinant,
            cov_a / determinant,
            opacity,
            colors[0],
            colors[1],
            colors[2],
        ]
    )


def render(attrs, is_live, pixel_x, pixel_y):
    diff_x = pixel_x[None, :] - attrs[0][:, None]
    diff_y = pixel_y[None, :] - attrs[1][:, None]
    power = -0.5 * (
        attrs[2][:, None] * diff_x * diff_x
        + 2.0 * attrs[3][:, None] * diff_x * diff_y
        + attrs[4][:, None] * diff_y * diff_y
    )
    alpha = jnp.where(is_live[:, None], attrs[5][:, None] * jnp.exp(power), 0.0)
    keeping = jnp.cumprod(1.0 - alpha, axis=0)
    transmit = jnp.concatenate([jnp.ones((1, alpha.shape[1]), alpha.dtype), keeping[:-1]], axis=0)
    return jnp.dot(attrs[6:9], alpha * transmit, precision=HIGH)


def pixels(position):
    pixel_idx = jnp.arange(256)
    pixel_x = (16 * (position % WIN - WIN // 2) + pixel_idx % 16).astype(jnp.float32) + 0.5
    pixel_y = (16 * (position // WIN - WIN // 2) + pixel_idx // 16).astype(jnp.float32) + 0.5
    return (pixel_x, pixel_y)


def tile_grads(row_vals, camcol, is_live, pixel_x, pixel_y, target):

    def loss_of(params_in):
        picture = render(project(params_in, camcol[:, None]), is_live, pixel_x, pixel_y)
        return (0.5 * jnp.sum((picture - target) ** 2), picture)

    loss_val, pullback, picture = jax.vjp(loss_of, row_vals, has_aux=True)
    return (picture, pullback(jnp.ones_like(loss_val))[0])


def camera_columns(cams, camera_ids):
    selector = (camera_ids[None, :] == jnp.arange(cams.shape[1])[:, None]).astype(jnp.float32)
    return jnp.dot(cams, selector, precision=HIGH)


def one_tile(rows_in, live_in, camcol, pos_x, pos_y, target):
    return tile_grads(
        fix_rows(rows_in.astype(jnp.float32), live_in), camcol, live_in, pos_x, pos_y, target
    )


def on_device(params, lists, tile_pos, cam_index, cams, targets):
    owners = lax.axis_size("gauss")
    g_dev = params.shape[1]
    width = params.shape[0]
    n_tiles, list_len = lists.shape
    capacity = n_tiles * list_len // owners
    flat_ids = lists.reshape(-1)
    is_live = flat_ids >= 0
    owner_idx = jnp.where(is_live, flat_ids // g_dev, owners)
    selector = (owner_idx[:, None] == jnp.arange(owners)[None, :]).astype(jnp.int32)
    ranks = jnp.sum((jnp.cumsum(selector, axis=0) - selector) * selector, axis=1)
    slot_pos = jnp.where(is_live, owner_idx * capacity + ranks, owners * capacity)
    read_pos = jnp.minimum(slot_pos, owners * capacity - 1)
    local_idx = jnp.where(is_live, flat_ids % g_dev, -1)
    tile_cams = camera_columns(cams, cam_index)
    pixel_x, pixel_y = jax.vmap(pixels)(tile_pos)
    tile_live = is_live.reshape(n_tiles, list_len)
    wanted = (
        jnp.full((owners * capacity,), -1, jnp.int32)
        .at[slot_pos]
        .set(local_idx, mode="drop")
        .reshape(owners, capacity)
    )
    received = lax.all_to_all(wanted, "gauss", split_axis=0, concat_axis=0, tiled=True).reshape(-1)
    received_live = received >= 0
    picked = jnp.take(params, jnp.maximum(received, 0), axis=1)
    returned = lax.all_to_all(
        picked.reshape(width, owners, capacity), "gauss", split_axis=1, concat_axis=1, tiled=True
    )
    slot_rows = jnp.take(returned.reshape(width, -1), read_pos, axis=1).reshape(
        width, n_tiles, list_len
    )
    pictures, tile_g = jax.vmap(one_tile, in_axes=(1, 0, 1, 0, 0, 1), out_axes=(1, 1))(
        slot_rows, tile_live, tile_cams, pixel_x, pixel_y, targets
    )
    slot_g = tile_g.reshape(width, -1)
    sent_g = (
        jnp.zeros((width, owners * capacity), jnp.float32).at[:, slot_pos].set(slot_g, mode="drop")
    )
    row_g = lax.all_to_all(
        sent_g.reshape(width, owners, capacity), "gauss", split_axis=1, concat_axis=1, tiled=True
    ).reshape(width, -1)
    targets_idx = jnp.where(received_live, received, g_dev)
    summed = jnp.zeros((width, g_dev), jnp.float32).at[:, targets_idx].add(row_g, mode="drop")
    grads = lax.psum(summed, "view")
    return (pictures, grads)


def solution(mesh):
    return jax.shard_map(
        on_device,
        mesh=mesh,
        in_specs=(
            P(None, "gauss"),
            P(("gauss", "view"), None),
            P(("gauss", "view")),
            P(("gauss", "view")),
            P(),
            P(None, ("gauss", "view"), None),
        ),
        out_specs=(P(None, ("gauss", "view"), None), P(None, "gauss")),
        check_vma=False,
    )
```

profile of v0, /device:TPU:1, one launch (start us, length us, event | category | flops | bytes accessed | tf_op | source)
XLA Modules:
  0.0 216.0 jit_solution(6644110838534625728)
XLA Ops:
  8.7 2.4 %scatter_custom_fusion = s32[512]{0:T(512)S(1)} fusion(s32[512]{0:T(512)S(1)} %bitcast.784, s32[512]{0:T(512)S(1)} %get-tuple-element.304, s32[]{:T(128)} %constant.170.clone.1), kind=kCustom, calls=%fused_computation.691 | custom fusion | bytes 2052 | tf_op jit(solution)/shard_map/scatter | solution.py:196
  11.9 20.5 %all-to-all-start = ((s32[128,1,4]{2,1,0:T(1,128)}), s32[128,1,4]{2,1,0:T(1,128)S(1)}, u32[]{:S(2)}, u32[]{:S(2)}) async-start(s32[128,1,4]{2,1,0:T(1,128)} %bitcast.8), calls=%async_computation | async-start | bytes 131072 | tf_op jit(solution)/shard_map/all_to_all | solution.py:199
  32.6 1.0 slice_reduce_fusion.15
  35.1 12.2 %all-to-all-done = s32[128,1,4]{2,1,0:T(1,128)S(1)} async-done(((s32[128,1,4]{2,1,0:T(1,128)}), s32[128,1,4]{2,1,0:T(1,128)S(1)}, u32[]{:S(2)}, u32[]{:S(2)}) %all-to-all-start) | async-done | bytes 2080 | tf_op jit(solution)/shard_map/all_to_all | solution.py:199
  49.5 1.3 gather_fusion
  51.8 5.7 %all-to-all-start.1 = ((bf16[128,2,128]{2,1,0:T(2,128)(2,1)}), bf16[128,2,128]{2,1,0:T(2,128)(2,1)S(1)}, u32[]{:S(2)}, u32[]{:S(2)}) async-start(bf16[128,2,128]{2,1,0:T(2,128)(2,1)} %reshape.12609), calls=%async_computation.1 | async-start | bytes 131072 | tf_op jit(solution)/shard_map/all_to_all | solution.py:202
  57.8 14.7 %all-to-all-done.1 = bf16[128,2,128]{2,1,0:T(2,128)(2,1)S(1)} async-done(((bf16[128,2,128]{2,1,0:T(2,128)(2,1)}), bf16[128,2,128]{2,1,0:T(2,128)(2,1)S(1)}, u32[]{:S(2)}, u32[]{:S(2)}) %all-to-all-start.1) | async-done | bytes 65568 | tf_op jit(solution)/shard_map/all_to_all | solution.py:202
  72.7 1.3 gather_fusion.1
  94.9 1.1 fusion.23
  96.0 1.8 fusion.22
  99.4 0.9 copy-done.12
  101.4 0.8 copy-done.2
  112.7 0.8 copy-done.20
  113.7 0.8 copy-done.9
  114.6 0.9 copy-done.7
  117.6 0.8 copy-done.17
  119.3 1.5 fusion.13
  123.9 0.9 multiply_multiply_fusion.26
  130.2 1.9 scatter_custom_fusion.1
  132.3 21.8 %all_to_all.19 = f32[128,1,256]{2,1,0:T(1,128)S(1)} all-to-all(f32[128,1,256]{2,1,0:T(1,128)S(1)} %reshape.12611), channel_id=1, replica_groups=mesh['gauss'=128,'view'=4] {'gauss'}, dimensions={0} | all-to-all | bytes 262144 | tf_op jit(solution)/shard_map/all_to_all | solution.py:215
  154.7 1.0 reduce.62
  155.8 3.2 %scatter_custom_fusion.2 = f32[64,1024]{0,1:T(8,128)} fusion(s32[512]{0:T(512)} %bitcast.783, f32[512,64]{1,0:T(8,128)S(1)} %bitcast.772, f32[]{:T(128)} %constant.184.clone.1), kind=kCustom, calls=%fused_computation.47 | custom fusion | flops 32768 | bytes 262656 | tf_op jit(solution)/shard_map/scatter-add | solution.py:219
  160.3 47.0 %all-reduce.139.cloned.1.call-done = f32[64,1024]{0,1:T(8,128)} async-done(((f32[64,1024]{0,1:T(8,128)}), f32[64,1024]{0,1:T(8,128)}) %all-reduce.139.cloned.1.call-update) | async-done | bytes 262160 | tf_op jit(solution)/shard_map/psum | solution.py:220
  207.2 1.9 copy.288
  (612 shorter events, 52.8 us)
Async XLA Ops:
  7.9 69.9 %copy-start.94 = (pred[4,128]{1,0:T(4,128)(4,1)}, pred[4,128]{1,0:T(4,128)(4,1)S(1)}, u32[]{:S(2)}) copy-start(pred[4,128]{1,0:T(4,128)(4,1)S(1)} %get-tuple-element.152) | copy-start | bytes 1540
  11.9 35.3 %all-to-all-start = ((s32[128,1,4]{2,1,0:T(1,128)}), s32[128,1,4]{2,1,0:T(1,128)S(1)}, u32[]{:S(2)}, u32[]{:S(2)}) async-start(s32[128,1,4]{2,1,0:T(1,128)} %bitcast.8), calls=%async_computation | async-start | bytes 131072 | tf_op jit(solution)/shard_map/all_to_all | solution.py:199
  33.6 42.5 %copy-start.56 = (f32[4]{0:T(128)}, f32[4]{0:T(128)S(1)}, u32[]{:S(2)}) copy-start(f32[4]{0:T(128)S(1)} %get-tuple-element.47) | copy-start | bytes 52
  33.6 42.5 %copy-start.63 = (f32[4]{0:T(128)}, f32[4]{0:T(128)S(1)}, u32[]{:S(2)}) copy-start(f32[4]{0:T(128)S(1)} %get-tuple-element.48) | copy-start | bytes 52
  33.6 42.5 %copy-start.138 = (f32[4]{0:T(128)}, f32[4]{0:T(128)S(1)}, u32[]{:S(2)}) copy-start(f32[4]{0:T(128)S(1)} %get-tuple-element.46) | copy-start | bytes 52
  33.6 43.6 %copy-start.85 = (f32[4]{0:T(128)}, f32[4]{0:T(128)S(1)}, u32[]{:S(2)}) copy-start(f32[4]{0:T(128)S(1)} %get-tuple-element.31) | copy-start | bytes 52
  34.0 42.2 %copy-start.58 = (f32[4]{0:T(128)}, f32[4]{0:T(128)S(1)}, u32[]{:S(2)}) copy-start(f32[4]{0:T(128)S(1)} %get-tuple-element.55) | copy-start | bytes 52
  34.0 42.2 %copy-start.61 = (f32[4]{0:T(128)}, f32[4]{0:T(128)S(1)}, u32[]{:S(2)}) copy-start(f32[4]{0:T(128)S(1)} %get-tuple-element.51) | copy-start | bytes 52
  34.0 42.2 %copy-start.65 = (f32[4]{0:T(128)}, f32[4]{0:T(128)S(1)}, u32[]{:S(2)}) copy-start(f32[4]{0:T(128)S(1)} %get-tuple-element.56) | copy-start | bytes 52
  34.0 42.2 %copy-start.68 = (f32[4]{0:T(128)}, f32[4]{0:T(128)S(1)}, u32[]{:S(2)}) copy-start(f32[4]{0:T(128)S(1)} %get-tuple-element.57) | copy-start | bytes 52
  34.0 42.2 %copy-start.71 = (f32[4]{0:T(128)}, f32[4]{0:T(128)S(1)}, u32[]{:S(2)}) copy-start(f32[4]{0:T(128)S(1)} %get-tuple-element.50) | copy-start | bytes 52
  34.0 42.2 %copy-start.73 = (f32[4]{0:T(128)}, f32[4]{0:T(128)S(1)}, u32[]{:S(2)}) copy-start(f32[4]{0:T(128)S(1)} %get-tuple-element.53) | copy-start | bytes 52
  34.0 42.2 %copy-start.83 = (f32[4]{0:T(128)}, f32[4]{0:T(128)S(1)}, u32[]{:S(2)}) copy-start(f32[4]{0:T(128)S(1)} %get-tuple-element.52) | copy-start | bytes 52
  34.0 42.2 %copy-start.140 = (f32[4]{0:T(128)}, f32[4]{0:T(128)S(1)}, u32[]{:S(2)}) copy-start(f32[4]{0:T(128)S(1)} %get-tuple-element.54) | copy-start | bytes 52
  34.0 42.2 %copy-start.143 = (f32[4]{0:T(128)}, f32[4]{0:T(128)S(1)}, u32[]{:S(2)}) copy-start(f32[4]{0:T(128)S(1)} %get-tuple-element.49) | copy-start | bytes 52
  34.8 41.5 %copy-start.196 = (f32[4]{0:T(128)}, f32[4]{0:T(128)S(1)}, u32[]{:S(2)}) copy-start(f32[4]{0:T(128)S(1)} %broadcast_multiply_fusion.24) | copy-start | bytes 52
  34.8 41.5 %copy-start.185 = (f32[4]{0:T(128)}, f32[4]{0:T(128)S(1)}, u32[]{:S(2)}) copy-start(f32[4]{0:T(128)S(1)} %get-tuple-element.308) | copy-start | bytes 52
  34.8 41.5 %copy-start.187 = (f32[4]{0:T(128)}, f32[4]{0:T(128)S(1)}, u32[]{:S(2)}) copy-start(f32[4]{0:T(128)S(1)} %get-tuple-element.309) | copy-start | bytes 52
  34.8 41.5 %copy-start.189 = (f32[4]{0:T(128)}, f32[4]{0:T(128)S(1)}, u32[]{:S(2)}) copy-start(f32[4]{0:T(128)S(1)} %get-tuple-element.310) | copy-start | bytes 52
  34.8 41.5 %copy-start.191 = (f32[4]{0:T(128)}, f32[4]{0:T(128)S(1)}, u32[]{:S(2)}) copy-start(f32[4]{0:T(128)S(1)} %get-tuple-element.311) | copy-start | bytes 52
  34.8 41.5 %copy-start.192 = (f32[4]{0:T(128)}, f32[4]{0:T(128)S(1)}, u32[]{:S(2)}) copy-start(f32[4]{0:T(128)S(1)} %get-tuple-element.312) | copy-start | bytes 52
  34.9 41.5 %copy-start.193 = (f32[4]{0:T(128)}, f32[4]{0:T(128)S(1)}, u32[]{:S(2)}) copy-start(f32[4]{0:T(128)S(1)} %get-tuple-element.313) | copy-start | bytes 52
  51.8 20.8 %all-to-all-start.1 = ((bf16[128,2,128]{2,1,0:T(2,128)(2,1)}), bf16[128,2,128]{2,1,0:T(2,128)(2,1)S(1)}, u32[]{:S(2)}, u32[]{:S(2)}) async-start(bf16[128,2,128]{2,1,0:T(2,128)(2,1)} %reshape.12609), calls=%async_computation.1 | async-start | bytes 131072 | tf_op jit(solution)/shard_map/all_to_all | solution.py:202
  57.5 149.7 %all-reduce.139.cloned.1.call-start = ((), (), s32[]{:S(2)}) async-start(), calls=%async_computation.3 | async-start | bytes 1048576 | tf_op jit(solution)/shard_map/psum | solution.py:220
  (183 other events, 393.5 us)
Sparse Core Ops, SparseCore 0:
  159.1 48.0 all-reduce.138
where the time goes:
time: 219 us; the launch traced here: 216 us
  waiting for transfers between devices  73.9 us (34%)
  local copies, waits for them, and re-layouts  54.9 us (25%)
  starting transfers between devices  26.4 us (12%)
  blocking collectives  21.8 us (10%)
  other arithmetic  18.4 us (8%)
  between operations  16.9 us (8%)
  matrix products  3.73 us (2%)
    psum x1, waiting for transfers between devices, on_device(): grads = lax.psum(summed, 'view')  47 us
    unnamed x411, local copies, waits for them, and re-layouts  38.7 us
    all_to_all x1, blocking collectives, on_device(): lax.all_to_all(sent_g.reshape(width, owners, capacity), 'gauss', split_ax...  21.8 us
    all_to_all x1, starting transfers between devices, on_device(): lax.all_to_all(wanted, 'gauss', split_axis=0, concat_axis=0, tiled=True)  20.5 us
    all_to_all x1, waiting for transfers between devices, on_device(): lax.all_to_all(picked.reshape(width, owners, capacity), 'gauss', split_ax...  14.7 us
    all_to_all x1, waiting for transfers between devices, on_device(): lax.all_to_all(wanted, 'gauss', split_axis=0, concat_axis=0, tiled=True)  12.2 us
    all_to_all x1, starting transfers between devices, on_device(): lax.all_to_all(picked.reshape(width, owners, capacity), 'gauss', split_ax...  5.7 us
  transfers between devices with their start and end apart: 3, of which 3 were waited for; matrix products, arithmetic and copies ran while one was open for 1% of the time, Pallas kernels for 0%

commit v1 on v0

--- a/solution.py
+++ b/solution.py
@@ -1,12 +1,11 @@
 import jax
 import jax.numpy as jnp
 from jax import lax
+from jax.experimental import pallas as pl
+from jax.experimental.pallas import tpu as pltpu
 from jax.sharding import PartitionSpec as P
 
 WIN = 16
-
-
-HIGH = lax.Precision.HIGHEST
 
 
 def sh_terms(dir_x, dir_y, dir_z):
@@ -30,10 +29,6 @@
     ]
 
 
-def fix_rows(row_vals, is_live):
-    return row_vals.at[6].set(jnp.where(is_live, row_vals[6], 1.0))
-
-
 def project(row_vals, camcols):
     mean_x, mean_y, mean_z = (row_vals[0], row_vals[1], row_vals[2])
     cam_rot = [camcols[index] for index in range(9)]
@@ -43,7 +38,12 @@
     cam_z = cam_rot[6] * mean_x + cam_rot[7] * mean_y + cam_rot[8] * mean_z + camcols[11]
     inv_z = 1.0 / cam_z
     quaternion = row_vals[6:10]
-    q_norm = jnp.sqrt(jnp.sum(quaternion * quaternion, axis=0))
+    q_norm = jnp.sqrt(
+        quaternion[0] * quaternion[0]
+        + quaternion[1] * quaternion[1]
+        + quaternion[2] * quaternion[2]
+        + quaternion[3] * quaternion[3]
+    )
     unit_w = quaternion[0] / q_norm
     unit_x = quaternion[1] / q_norm
     unit_y = quaternion[2] / q_norm
@@ -83,7 +83,7 @@
         jac_scale * mixed[1][col_k] - jac_scale * cam_y * inv_z * mixed[2][col_k]
         for col_k in range(3)
     ]
-    var_diag = jnp.exp(2.0 * row_vals[3:6])
+    var_diag = [jnp.exp(2.0 * row_vals[axis]) for axis in range(3, 6)]
     cov_a = (
         proj_u[0] * proj_u[0] * var_diag[0]
         + proj_u[1] * proj_u[1] * var_diag[1]
@@ -116,9 +116,8 @@
         colors.append(shade)
     centre_u = focal * cam_x * inv_z
     centre_v = focal * cam_y * inv_z
-    return jnp.stack(
-        [
-            centre_u,
+    return [
+        centre_u,
             centre_v,
             cov_c / determinant,
             -cov_b / determinant,
@@ -127,50 +126,233 @@
             colors[0],
             colors[1],
             colors[2],
-        ]
-    )
-
-
-def render(attrs, is_live, pixel_x, pixel_y):
-    diff_x = pixel_x[None, :] - attrs[0][:, None]
-    diff_y = pixel_y[None, :] - attrs[1][:, None]
-    power = -0.5 * (
-        attrs[2][:, None] * diff_x * diff_x
-        + 2.0 * attrs[3][:, None] * diff_x * diff_y
-        + attrs[4][:, None] * diff_y * diff_y
-    )
-    alpha = jnp.where(is_live[:, None], attrs[5][:, None] * jnp.exp(power), 0.0)
-    keeping = jnp.cumprod(1.0 - alpha, axis=0)
-    transmit = jnp.concatenate([jnp.ones((1, alpha.shape[1]), alpha.dtype), keeping[:-1]], axis=0)
-    return jnp.dot(attrs[6:9], alpha * transmit, precision=HIGH)
-
-
-def pixels(position):
-    pixel_idx = jnp.arange(256)
-    pixel_x = (16 * (position % WIN - WIN // 2) + pixel_idx % 16).astype(jnp.float32) + 0.5
-    pixel_y = (16 * (position // WIN - WIN // 2) + pixel_idx // 16).astype(jnp.float32) + 0.5
-    return (pixel_x, pixel_y)
-
-
-def tile_grads(row_vals, camcol, is_live, pixel_x, pixel_y, target):
-
-    def loss_of(params_in):
-        picture = render(project(params_in, camcol[:, None]), is_live, pixel_x, pixel_y)
-        return (0.5 * jnp.sum((picture - target) ** 2), picture)
-
-    loss_val, pullback, picture = jax.vjp(loss_of, row_vals, has_aux=True)
-    return (picture, pullback(jnp.ones_like(loss_val))[0])
-
-
-def camera_columns(cams, camera_ids):
-    selector = (camera_ids[None, :] == jnp.arange(cams.shape[1])[:, None]).astype(jnp.float32)
-    return jnp.dot(cams, selector, precision=HIGH)
-
-
-def one_tile(rows_in, live_in, camcol, pos_x, pos_y, target):
-    return tile_grads(
-        fix_rows(rows_in.astype(jnp.float32), live_in), camcol, live_in, pos_x, pos_y, target
-    )
+    ]
+
+
+def tile_values(scalars, shape):
+    tile = lax.broadcasted_iota(jnp.int32, shape, 0) % len(scalars)
+    out = jnp.full(shape, scalars[0])
+    for index, value in enumerate(scalars[1:], 1):
+        out = jnp.where(tile == index, value, out)
+    return out
+
+
+def render_kernel(
+    rows_ref, ids_ref, pos_ref, cam_ref, cams_ref, target_ref,
+    picture_ref, grads_ref,
+    dx_s, dy_s, exp_s, alpha_s, trans_s, color_s,
+):
+    n_tiles, slots = ids_ref.shape
+    half = target_ref.shape[2] // 2
+    wide = (2 * n_tiles, half)
+    narrow = (n_tiles, slots)
+    live = ids_ref[...] >= 0
+    camcols = [
+        tile_values([cams_ref[row, cam_ref[t]] for t in range(n_tiles)], narrow)
+        for row in range(cams_ref.shape[0])
+    ]
+    row_vals = [rows_ref[row].astype(jnp.float32) for row in range(rows_ref.shape[0])]
+    row_vals[6] = jnp.where(live, row_vals[6], 1.0)
+    attrs, pullback = jax.vjp(lambda vals: project(vals, camcols), row_vals)
+    attrs_live = list(attrs)
+    for index in range(2, 6):
+        attrs_live[index] = jnp.where(live, attrs[index], 0.0)
+    attrs8 = [jnp.concatenate([a, a], axis=0) for a in attrs_live]
+
+    row_id = lax.broadcasted_iota(jnp.int32, wide, 0)
+    lane = lax.broadcasted_iota(jnp.int32, wide, 1)
+    pixel = lane + jnp.where(row_id >= n_tiles, half, 0)
+    base_x = tile_values([16 * (pos_ref[t] % WIN - WIN // 2) for t in range(n_tiles)], wide)
+    base_y = tile_values([16 * (pos_ref[t] // WIN - WIN // 2) for t in range(n_tiles)], wide)
+    pixel_x = (base_x + pixel % 16).astype(jnp.float32) + 0.5
+    pixel_y = (base_y + pixel // 16).astype(jnp.float32) + 0.5
+
+    def spread(values, slot):
+        at = jnp.full(wide, slot, jnp.int32)
+        return jnp.take_along_axis(values, at, axis=1, mode="promise_in_bounds")
+
+    unroll = 8
+
+    def forward(step, carry):
+        trans, r0, r1, r2 = carry
+        for inner in range(unroll):
+            slot = step * unroll + inner
+            u, v, ca, cb, cc, op, c0, c1, c2 = [spread(a, slot) for a in attrs8]
+            dx = pixel_x - u
+            dy = pixel_y - v
+            power = -0.5 * (ca * dx * dx + 2.0 * cb * dx * dy + cc * dy * dy)
+            e = jnp.exp(power)
+            alpha = op * e
+            dx_s[slot] = dx
+            dy_s[slot] = dy
+            exp_s[slot] = e
+            alpha_s[slot] = alpha
+            trans_s[slot] = trans
+            color_s[0, slot] = c0
+            color_s[1, slot] = c1
+            color_s[2, slot] = c2
+            w = alpha * trans
+            r0, r1, r2 = r0 + c0 * w, r1 + c1 * w, r2 + c2 * w
+            trans = trans * (1.0 - alpha)
+        return trans, r0, r1, r2
+
+    zero = jnp.zeros(wide, jnp.float32)
+    _, r0, r1, r2 = lax.fori_loop(
+        0, slots // unroll, forward, (jnp.ones(wide, jnp.float32), zero, zero, zero)
+    )
+    res = []
+    for chan, pic in enumerate((r0, r1, r2)):
+        picture_ref[chan, :, :half] = pic[:n_tiles]
+        picture_ref[chan, :, half:] = pic[n_tiles:]
+        want = target_ref[chan]
+        res.append(pic - jnp.concatenate([want[:, :half], want[:, half:]], axis=0))
+
+    def backward(step, carry):
+        behind, accs = carry
+        accs = list(accs)
+        for inner in range(unroll):
+            slot = slots - 1 - (step * unroll + inner)
+            dx, dy, e, alpha, trans = dx_s[slot], dy_s[slot], exp_s[slot], alpha_s[slot], trans_s[slot]
+            q = color_s[0, slot] * res[0] + color_s[1, slot] * res[1] + color_s[2, slot] * res[2]
+            w = alpha * trans
+            diff = q - behind
+            gain = trans * diff * e
+            behind = behind + alpha * diff
+            gx = gain * dx
+            gy = gain * dy
+            terms = [gain, gx, gy, gx * dx, gx * dy, gy * dy, w * res[0], w * res[1], w * res[2]]
+            here = lane == slot
+            for index, term in enumerate(terms):
+                total = jnp.sum(term, axis=1, keepdims=True)
+                accs[index] = jnp.where(here, total, accs[index])
+        return behind, tuple(accs)
+
+    _, accs = lax.fori_loop(0, slots // unroll, backward, (zero, (zero,) * 9))
+    g0, gx, gy, gxx, gxy, gyy, k0, k1, k2 = [a[:n_tiles] + a[n_tiles:] for a in accs]
+    op = attrs_live[5]
+    ca, cb, cc = attrs_live[2:5]
+    cot = [
+        op * (ca * gx + cb * gy),
+        op * (cb * gx + cc * gy),
+        -0.5 * (op * gxx),
+        -(op * gxy),
+        -0.5 * (op * gyy),
+        g0,
+        k0,
+        k1,
+        k2,
+    ]
+    cot = [jnp.where(live, value, 0.0) for value in cot]
+    (grads,) = pullback(cot)
+    for row, value in enumerate(grads):
+        grads_ref[row] = value
+
+
+def render_call(rows, lists, tile_pos, cam_index, cams, targets, interpret=False):
+    width = rows.shape[0]
+    n_tiles, slots = lists.shape
+    lanes = targets.shape[2] // 2
+    vmem = pl.BlockSpec(memory_space=pltpu.VMEM)
+    smem = pl.BlockSpec(memory_space=pltpu.SMEM)
+    plane = pltpu.VMEM((slots, 2 * n_tiles, lanes), jnp.float32)
+    return pl.pallas_call(
+        render_kernel,
+        out_shape=(
+            jax.ShapeDtypeStruct(targets.shape, jnp.float32),
+            jax.ShapeDtypeStruct((width, n_tiles, slots), jnp.float32),
+        ),
+        in_specs=[vmem, vmem, smem, smem, smem, vmem],
+        out_specs=(vmem, vmem),
+        scratch_shapes=[plane] * 5
+        + [pltpu.VMEM((3, slots, 2 * n_tiles, lanes), jnp.float32)],
+        interpret=interpret,
+    )(rows, lists, tile_pos, cam_index, cams, targets)
+
+
+def reduce_kernel(n_view, idx_ref, rows_ref, out_ref, local, arrived, gathered, sem_a, sem_b):
+    me = lax.axis_index("view")
+    width, g_dev = out_ref.shape
+    chunk = width // n_view
+    barrier = pltpu.get_barrier_semaphore()
+    for step in range(1, n_view):
+        pl.semaphore_signal(
+            barrier,
+            inc=1,
+            device_id={"view": lax.rem(me + step, n_view)},
+            device_id_type=pl.DeviceIdType.MESH,
+        )
+    n_idx = idx_ref.shape[1]
+    hot = jnp.where(
+        lax.broadcasted_iota(jnp.int32, (g_dev, n_idx), 0) == idx_ref[...], 1.0, 0.0
+    ).astype(jnp.bfloat16)
+    rest = rows_ref[...]
+    total = jnp.zeros((width, g_dev), jnp.float32)
+    for _ in range(3):
+        piece = rest.astype(jnp.bfloat16)
+        rest = rest - piece.astype(jnp.float32)
+        total = total + lax.dot_general(
+            piece, hot, (((1,), (1,)), ((), ())), preferred_element_type=jnp.float32
+        )
+    local[...] = total.reshape(n_view, chunk, g_dev)
+    pl.semaphore_wait(barrier, n_view - 1)
+    first = []
+    for step in range(1, n_view):
+        peer = lax.rem(me + step, n_view)
+        copy = pltpu.make_async_remote_copy(
+            src_ref=local.at[peer],
+            dst_ref=arrived.at[step - 1],
+            send_sem=sem_a.at[0, step - 1],
+            recv_sem=sem_a.at[1, step - 1],
+            device_id={"view": peer},
+            device_id_type=pl.DeviceIdType.MESH,
+        )
+        copy.start()
+        first.append(copy)
+    for copy in first:
+        copy.wait()
+    mine = local[me]
+    for step in range(1, n_view):
+        mine = mine + arrived[step - 1]
+    gathered[0] = mine
+    second = []
+    for step in range(1, n_view):
+        peer = lax.rem(me + step, n_view)
+        copy = pltpu.make_async_remote_copy(
+            src_ref=gathered.at[0],
+            dst_ref=gathered.at[step],
+            send_sem=sem_b.at[0, step - 1],
+            recv_sem=sem_b.at[1, step - 1],
+            device_id={"view": peer},
+            device_id_type=pl.DeviceIdType.MESH,
+        )
+        copy.start()
+        second.append(copy)
+    for copy in second:
+        copy.wait()
+    for step in range(n_view):
+        origin = lax.rem(me + n_view - step, n_view)
+        out_ref[pl.ds(pl.multiple_of(origin * chunk, chunk), chunk)] = gathered[step]
+
+
+def reduce_call(idx, rows, g_dev):
+    n_view = lax.axis_size("view")
+    width = rows.shape[0]
+    chunk = width // n_view
+    vmem = pl.BlockSpec(memory_space=pltpu.VMEM)
+    return pl.pallas_call(
+        lambda *refs: reduce_kernel(n_view, *refs),
+        out_shape=jax.ShapeDtypeStruct((width, g_dev), jnp.float32),
+        in_specs=[vmem, vmem],
+        out_specs=vmem,
+        scratch_shapes=[
+            pltpu.VMEM((n_view, chunk, g_dev), jnp.float32),
+            pltpu.VMEM((n_view - 1, chunk, g_dev), jnp.float32),
+            pltpu.VMEM((n_view, chunk, g_dev), jnp.float32),
+            pltpu.SemaphoreType.DMA((2, n_view - 1)),
+            pltpu.SemaphoreType.DMA((2, n_view - 1)),
+        ],
+        compiler_params=pltpu.CompilerParams(collective_id=0, has_side_effects=True),
+    )(idx, rows)
 
 
 def on_device(params, lists, tile_pos, cam_index, cams, targets):
@@ -187,9 +369,6 @@
     slot_pos = jnp.where(is_live, owner_idx * capacity + ranks, owners * capacity)
     read_pos = jnp.minimum(slot_pos, owners * capacity - 1)
     local_idx = jnp.where(is_live, flat_ids % g_dev, -1)
-    tile_cams = camera_columns(cams, cam_index)
-    pixel_x, pixel_y = jax.vmap(pixels)(tile_pos)
-    tile_live = is_live.reshape(n_tiles, list_len)
     wanted = (
         jnp.full((owners * capacity,), -1, jnp.int32)
         .at[slot_pos]
@@ -197,7 +376,6 @@
         .reshape(owners, capacity)
     )
     received = lax.all_to_all(wanted, "gauss", split_axis=0, concat_axis=0, tiled=True).reshape(-1)
-    received_live = received >= 0
     picked = jnp.take(params, jnp.maximum(received, 0), axis=1)
     returned = lax.all_to_all(
         picked.reshape(width, owners, capacity), "gauss", split_axis=1, concat_axis=1, tiled=True
@@ -205,9 +383,7 @@
     slot_rows = jnp.take(returned.reshape(width, -1), read_pos, axis=1).reshape(
         width, n_tiles, list_len
     )
-    pictures, tile_g = jax.vmap(one_tile, in_axes=(1, 0, 1, 0, 0, 1), out_axes=(1, 1))(
-        slot_rows, tile_live, tile_cams, pixel_x, pixel_y, targets
-    )
+    pictures, tile_g = render_call(slot_rows, lists, tile_pos, cam_index, cams, targets)
     slot_g = tile_g.reshape(width, -1)
     sent_g = (
         jnp.zeros((width, owners * capacity), jnp.float32).at[:, slot_pos].set(slot_g, mode="drop")
@@ -215,9 +391,7 @@
     row_g = lax.all_to_all(
         sent_g.reshape(width, owners, capacity), "gauss", split_axis=1, concat_axis=1, tiled=True
     ).reshape(width, -1)
-    targets_idx = jnp.where(received_live, received, g_dev)
-    summed = jnp.zeros((width, g_dev), jnp.float32).at[:, targets_idx].add(row_g, mode="drop")
-    grads = lax.psum(summed, "view")
+    grads = reduce_call(received.reshape(1, -1), row_g, g_dev)
     return (pictures, grads)
 
 

time: 219 us -> 121 us (0.55); the launches traced: 216 us -> 121 us
  local copies, waits for them, and re-layouts: 54.9 us -> 16.8 us
  waiting for transfers between devices: 73.9 us -> 43.8 us
  Pallas kernels: 0 us -> 23.2 us
  blocking collectives: 21.8 us -> 0 us
  between operations: 16.9 us -> 0.86 us
  other arithmetic: 18.4 us -> 4.22 us
  starting transfers between devices: 26.4 us -> 31.7 us
  matrix products: 3.73 us -> 0 us
    psum x1 -> x0, waiting for transfers between devices: 47 us -> none  [on_device(): grads = lax.psum(summed, 'view')]
    unnamed x411 -> x14, local copies, waits for them, and re-layouts: 38.7 us -> 5.11 us
    pallas_call x0 -> x2, Pallas kernels: none -> 23.2 us  [the longest x1 15.8 us: reduce_call(): pl.pallas_call(lambda *refs: reduce_kernel(n_view, *refs), out_shape=jax....]
    all_to_all x1 -> x0, blocking collectives: 21.8 us -> none  [on_device(): lax.all_to_all(sent_g.reshape(width, owners, capacity), 'gauss', split_ax...]
    all_to_all x0 -> x1, waiting for transfers between devices: none -> 15.5 us  [on_device(): lax.all_to_all(sent_g.reshape(width, owners, capacity), 'gauss', split_ax...]
    all_to_all x0 -> x1, starting transfers between devices: none -> 5.62 us  [on_device(): lax.all_to_all(sent_g.reshape(width, owners, capacity), 'gauss', split_ax...]
    mul x53 -> x0, other arithmetic: 4.96 us -> none  [the longest x30 2.67 us: render(): keeping = jnp.cumprod(1.0 - alpha, axis=0)]
    slice x38 -> x0, local copies, waits for them, and re-layouts: 4.24 us -> none  [the longest x35 2.78 us: render(): keeping = jnp.cumprod(1.0 - alpha, axis=0)]
where the time goes in v1:
time: 121 us
  waiting for transfers between devices  43.8 us (36%)
  starting transfers between devices  31.7 us (26%)
  Pallas kernels  23.2 us (19%)
  local copies, waits for them, and re-layouts  16.8 us (14%)
  other arithmetic  4.22 us (3%)
    all_to_all x1, starting transfers between devices, on_device(): lax.all_to_all(wanted, 'gauss', split_axis=0, concat_axis=0, tiled=True)  20.4 us
    pallas_call x1, Pallas kernels, reduce_call(): pl.pallas_call(lambda *refs: reduce_kernel(n_view, *refs), out_shape=jax....  15.8 us
    all_to_all x1, waiting for transfers between devices, on_device(): lax.all_to_all(sent_g.reshape(width, owners, capacity), 'gauss', split_ax...  15.5 us
    all_to_all x1, waiting for transfers between devices, on_device(): lax.all_to_all(wanted, 'gauss', split_axis=0, concat_axis=0, tiled=True)  14.6 us
    all_to_all x1, waiting for transfers between devices, on_device(): lax.all_to_all(picked.reshape(width, owners, capacity), 'gauss', split_ax...  13.7 us
    pallas_call x1, Pallas kernels, render_call(): pl.pallas_call(render_kernel, out_shape=(jax.ShapeDtypeStruct(targets.sha...  7.41 us
    all_to_all x1, starting transfers between devices, on_device(): lax.all_to_all(picked.reshape(width, owners, capacity), 'gauss', split_ax...  5.7 us
    all_to_all x1, starting transfers between devices, on_device(): lax.all_to_all(sent_g.reshape(width, owners, capacity), 'gauss', split_ax...  5.62 us
  transfers between devices with their start and end apart: 3, of which 3 were waited for; matrix products, arithmetic and copies ran while one was open for 1% of the time, Pallas kernels for 0%

profile of v1, /device:TPU:1, one launch (start us, length us, event | category | flops | bytes accessed | tf_op | source)
XLA Modules:
  0.0 120.6 jit_solution(13580185766219079962)
XLA Ops:
  0.6 0.8 fusion.8
  2.1 2.4 %scatter_custom_fusion = s32[512]{0:T(512)S(1)} fusion(s32[512]{0:T(512)S(1)} %bitcast.88, s32[512]{0:T(512)S(1)} %get-tuple-element.10, s32[]{:T(128)} %constant.66.clone.1), kind=kCustom, calls=%fused_computation.57 | custom fusion | bytes 2052 | tf_op jit(solution)/shard_map/scatter | solution.py:375
  4.6 0.7 all_to_all.12
  5.3 20.4 %all-to-all-start = ((s32[128,1,4]{2,1,0:T(1,128)}), s32[128,1,4]{2,1,0:T(1,128)S(1)}, u32[]{:S(2)}, u32[]{:S(2)}) async-start(s32[128,1,4]{2,1,0:T(1,128)} %bitcast.8), calls=%async_computation | async-start | bytes 131072 | tf_op jit(solution)/shard_map/all_to_all | solution.py:378
  25.9 14.6 %all-to-all-done = s32[128,1,4]{2,1,0:T(1,128)S(1)} async-done(((s32[128,1,4]{2,1,0:T(1,128)}), s32[128,1,4]{2,1,0:T(1,128)S(1)}, u32[]{:S(2)}, u32[]{:S(2)}) %all-to-all-start) | async-done | bytes 2080 | tf_op jit(solution)/shard_map/all_to_all | solution.py:378
  41.4 1.0 fusion.20
  42.5 1.3 %gather_fusion = bf16[512,64]{1,0:T(8,128)(2,1)S(1)} fusion(bf16[64,1024]{0,1:T(8,128)(2,1)S(1)} %copy.34, s32[1024]{0:T(1024)S(1)} %pad_clamp_fusion.1), kind=kCustom, calls=%fused_computation | custom fusion | bytes 133120 | tf_op jit(solution)/shard_map/jit(_take)/gather | solution.py:379
  44.1 0.7 reshape.293
  44.8 5.7 %all-to-all-start.1 = ((bf16[128,2,128]{2,1,0:T(2,128)(2,1)}), bf16[128,2,128]{2,1,0:T(2,128)(2,1)S(1)}, u32[]{:S(2)}, u32[]{:S(2)}) async-start(bf16[128,2,128]{2,1,0:T(2,128)(2,1)} %reshape.293), calls=%async_computation.1 | async-start | bytes 131072 | tf_op jit(solution)/shard_map/all_to_all | solution.py:380
  50.6 0.7 copy-done.2
  51.2 0.7 copy.36.cams_ref
  51.9 13.7 %all-to-all-done.1 = bf16[128,2,128]{2,1,0:T(2,128)(2,1)S(1)} async-done(((bf16[128,2,128]{2,1,0:T(2,128)(2,1)}), bf16[128,2,128]{2,1,0:T(2,128)(2,1)S(1)}, u32[]{:S(2)}, u32[]{:S(2)}) %all-to-all-start.1) | async-done | bytes 65568 | tf_op jit(solution)/shard_map/all_to_all | solution.py:380
  65.7 1.3 %gather_fusion.1 = bf16[512,64]{1,0:T(8,128)(2,1)S(1)} fusion(bf16[64,512]{0,1:T(8,128)(2,1)S(1)} %bitcast.75, s32[1024]{0:T(1024)S(1)} %pad_clamp_fusion), kind=kCustom, calls=%fused_computation.1 | custom fusion | bytes 133120 | tf_op jit(solution)/shard_map/jit(_take)/gather | solution.py:383
  67.8 7.4 %shard_map.77 = (f32[3,4,256]{2,1,0:T(4,128)}, f32[64,4,128]{2,1,0:T(4,128)}) custom-call(bf16[64,4,128]{2,1,0:T(4,128)(2,1)} %broadcast_select_fusion.1.rows_ref, s32[4,128]{1,0:T(4,128)} %ids_ref.1, s32[4]{0:T(128)} %pos_ref.1, s32[4]{0:T(128)} %cam_ref.1, f32[28,16]{1,0:T(8,128)} %copy.36.cams_ref, f32[3,4,256]{2,1,0:T(4,128)} %target_ref.1), custom_call_target="tpu_custom_call" | custom-call | tf_op jit(solution)/shard_map/pallas_call | solution.py:258
  75.2 1.0 copy.40
  76.2 1.8 %scatter_custom_fusion.1 = f32[64,512]{0,1:T(8,128)S(1)} fusion(s32[512]{0:T(512)S(1)} %bitcast.89, f32[512,64]{1,0:T(8,128)S(1)} %bitcast.82, f32[]{:T(128)} %constant.73.clone.1), kind=kCustom, calls=%fused_computation.11 | custom fusion | bytes 131076 | tf_op jit(solution)/shard_map/scatter | solution.py:389
  78.0 0.9 reshape.295
  78.9 5.6 %all-to-all-start.2 = ((f32[128,1,256]{2,1,0:T(1,128)}), f32[128,1,256]{2,1,0:T(1,128)S(1)}, u32[]{:S(2)}, u32[]{:S(2)}) async-start(f32[128,1,256]{2,1,0:T(1,128)} %reshape.295), calls=%async_computation.2 | async-start | bytes 262144 | tf_op jit(solution)/shard_map/all_to_all | solution.py:391
  84.6 0.7 reshape_reshape.3.refs_0_
  85.2 15.5 %all-to-all-done.2 = f32[128,1,256]{2,1,0:T(1,128)S(1)} async-done(((f32[128,1,256]{2,1,0:T(1,128)}), f32[128,1,256]{2,1,0:T(1,128)S(1)}, u32[]{:S(2)}, u32[]{:S(2)}) %all-to-all-start.2) | async-done | bytes 131104 | tf_op jit(solution)/shard_map/all_to_all | solution.py:391
  101.2 1.0 reduce.9
  102.4 0.8 copy.38.refs_1_
  103.1 15.8 %shard_map.78 = f32[64,1024]{1,0:T(8,128)} custom-call(s32[1,512]{1,0:T(1,128)} %reshape_reshape.3.refs_0_, f32[64,512]{1,0:T(8,128)} %copy.38.refs_1_), custom_call_target="tpu_custom_call" | custom-call | tf_op jit(solution)/shard_map/pallas_call | solution.py:342
  118.9 1.7 %copy.42 = f32[64,1024]{1,0:T(8,128)} copy(f32[64,1024]{1,0:T(8,128)} %shard_map.78) | data formatting | bytes 524288
  (32 shorter events, 3.6 us)
Async XLA Ops:
  0.6 0.8 copy-start.1
  2.1 23.6 %copy-start = (bf16[64,1024]{1,0:T(8,128)(2,1)S(1)}, bf16[64,1024]{1,0:T(8,128)(2,1)}, u32[]{:S(2)}) copy-start(bf16[64,1024]{1,0:T(8,128)(2,1)} %param.6) | copy-start | bytes 393220
  5.3 35.2 %all-to-all-start = ((s32[128,1,4]{2,1,0:T(1,128)}), s32[128,1,4]{2,1,0:T(1,128)S(1)}, u32[]{:S(2)}, u32[]{:S(2)}) async-start(s32[128,1,4]{2,1,0:T(1,128)} %bitcast.8), calls=%async_computation | async-start | bytes 131072 | tf_op jit(solution)/shard_map/all_to_all | solution.py:378
  44.8 20.8 %all-to-all-start.1 = ((bf16[128,2,128]{2,1,0:T(2,128)(2,1)}), bf16[128,2,128]{2,1,0:T(2,128)(2,1)S(1)}, u32[]{:S(2)}, u32[]{:S(2)}) async-start(bf16[128,2,128]{2,1,0:T(2,128)(2,1)} %reshape.293), calls=%async_computation.1 | async-start | bytes 131072 | tf_op jit(solution)/shard_map/all_to_all | solution.py:380
  50.5 0.7 copy-start.2
  78.9 21.8 %all-to-all-start.2 = ((f32[128,1,256]{2,1,0:T(1,128)}), f32[128,1,256]{2,1,0:T(1,128)S(1)}, u32[]{:S(2)}, u32[]{:S(2)}) async-start(f32[128,1,256]{2,1,0:T(1,128)} %reshape.295), calls=%async_computation.2 | async-start | bytes 262144 | tf_op jit(solution)/shard_map/all_to_all | solution.py:391

commit v2 on v1

--- a/solution.py
+++ b/solution.py
@@ -137,9 +137,8 @@
     return out
 
 
-def render_kernel(
-    rows_ref, ids_ref, pos_ref, cam_ref, cams_ref, target_ref,
-    picture_ref, grads_ref,
+def render_tiles(
+    rows_ref, ids_ref, pos_ref, cam_ref, cams_ref, target_ref, picture_ref,
     dx_s, dy_s, exp_s, alpha_s, trans_s, color_s,
 ):
     n_tiles, slots = ids_ref.shape
@@ -151,11 +150,11 @@
         tile_values([cams_ref[row, cam_ref[t]] for t in range(n_tiles)], narrow)
         for row in range(cams_ref.shape[0])
     ]
-    row_vals = [rows_ref[row].astype(jnp.float32) for row in range(rows_ref.shape[0])]
+    row_vals = [rows_ref[row] for row in range(rows_ref.shape[0])]
     row_vals[6] = jnp.where(live, row_vals[6], 1.0)
     attrs, pullback = jax.vjp(lambda vals: project(vals, camcols), row_vals)
     attrs_live = list(attrs)
-    for index in range(2, 6):
+    for index in range(9):
         attrs_live[index] = jnp.where(live, attrs[index], 0.0)
     attrs8 = [jnp.concatenate([a, a], axis=0) for a in attrs_live]
 
@@ -245,154 +244,241 @@
     cot = [jnp.where(live, value, 0.0) for value in cot]
     (grads,) = pullback(cot)
     for row, value in enumerate(grads):
-        grads_ref[row] = value
-
-
-def render_call(rows, lists, tile_pos, cam_index, cams, targets, interpret=False):
-    width = rows.shape[0]
+        rows_ref[row] = jnp.where(live, value, 0.0)
+
+
+CAP = 4
+
+
+def pieces(values):
+    out = []
+    for _ in range(3):
+        out.append(values.astype(jnp.bfloat16))
+        values = values - out[-1].astype(jnp.float32)
+    return out
+
+
+def dot(a, b, dims):
+    return lax.dot_general(a, b, (dims, ((), ())), preferred_element_type=jnp.float32)
+
+
+def step_kernel(
+    n_view, n_z, n_c,
+    params_ref, ids_ref, pos_ref, cam_ref, cams_ref, target_ref,
+    picture_ref, out_ref,
+    want_s, ask_a, ask_b, par_x, par_y, par_s, par_q, rows_s,
+    grad_s, grad_y, grad_x, grad_u, hot_s, pick_s,
+    dx_s, dy_s, exp_s, alpha_s, trans_s, color_s,
+    local, arrived, gathered,
+    sem_z, sem_c, sem_v,
+):
+    owners = n_z * n_c
+    width, g_dev = params_ref.shape
+    n_tiles, slots = ids_ref.shape
+    f32, bf16 = jnp.float32, jnp.bfloat16
+    me = lax.axis_index("gauss")
+    my_view = lax.axis_index("view")
+    my_z, my_c = me // n_c, lax.rem(me, n_c)
+
+    def z_peer(step):
+        other = lax.rem(my_z + step, n_z)
+        return other, {"gauss": other * n_c + my_c}
+
+    def c_peer(step):
+        other = lax.rem(my_c + step, n_c)
+        return other, {"gauss": my_z * n_c + other}
+
+    def v_peer(step):
+        other = lax.rem(my_view + step, n_view)
+        return other, {"view": other}
+
+    barrier = pltpu.get_barrier_semaphore()
+    for count, peer in ((n_z, z_peer), (n_c, c_peer), (n_view, v_peer)):
+        for step in range(1, count):
+            pl.semaphore_signal(
+                barrier, inc=1, device_id=peer(step)[1], device_id_type=pl.DeviceIdType.MESH
+            )
+
+    def exchange(count, peer, sems, phase, source, target):
+        copies = []
+        for step in range(1, count):
+            other, device = peer(step)
+            copy = pltpu.make_async_remote_copy(
+                src_ref=source(other),
+                dst_ref=target(step),
+                send_sem=sems.at[phase, 0, step - 1],
+                recv_sem=sems.at[phase, 1, step - 1],
+                device_id=device,
+                device_id_type=pl.DeviceIdType.MESH,
+            )
+            copy.start()
+            copies.append(copy)
+        return copies
+
+    def finish(copies):
+        for copy in copies:
+            copy.wait()
+
+    bits = g_dev.bit_length() - 1
+    own_row = lax.broadcasted_iota(jnp.int32, (owners, slots), 0)
+    lane = lax.broadcasted_iota(jnp.int32, (owners, slots), 1)
+    before = (
+        lax.broadcasted_iota(jnp.int32, (slots, slots), 0)
+        < lax.broadcasted_iota(jnp.int32, (slots, slots), 1)
+    )
+    before = jnp.where(before, 1.0, 0.0).astype(bf16)
+    seen = jnp.zeros((owners, 1), f32)
+    asked = [jnp.zeros((owners, slots), f32) for _ in range(CAP)]
+    for t in range(n_tiles):
+        ids = ids_ref[t : t + 1, :]
+        owner = lax.shift_right_arithmetic(ids, bits)
+        index = (lax.bitwise_and(ids, g_dev - 1) + 1).astype(f32)
+        named = own_row == owner
+        named_f = jnp.where(named, 1.0, 0.0)
+        rank = dot(named_f.astype(bf16), before, ((1,), (0,))) + seen
+        seen = seen + jnp.sum(named_f, axis=1, keepdims=True)
+        for c in range(CAP):
+            chosen = jnp.where(rank == float(c), named_f, 0.0)
+            pick_s[c, :, t * slots : (t + 1) * slots] = chosen.astype(bf16)
+            asked[c] = asked[c] + chosen * index
+    spread = jnp.zeros((owners, slots), f32)
+    for c in range(CAP):
+        column = jnp.sum(asked[c], axis=1, keepdims=True)
+        spread = spread + jnp.where(lane == lax.rem(own_row, n_c) * CAP + c, column, 0.0)
+    want = jnp.sum(spread.reshape(n_z, n_c, slots), axis=1)
+    for z in range(n_z):
+        want_s[z] = want[z : z + 1]
+    pl.semaphore_wait(barrier, n_z + n_c + n_view - 3)
+
+    copies = exchange(n_z, z_peer, sem_z, 0, lambda o: want_s.at[o], lambda s: ask_a.at[my_z])
+    ask_a[my_z] = want_s[my_z]
+    finish(copies)
+    copies = exchange(n_c, c_peer, sem_c, 0, lambda o: ask_a, lambda s: ask_b.at[my_c])
+    ask_b[my_c] = ask_a[...]
+    finish(copies)
+    asks = ask_b[...].reshape(owners, slots)
+    params = params_ref[...]
+    place = lax.broadcasted_iota(jnp.int32, (owners, g_dev), 1) + 1
+    answers = []
+    for c in range(CAP):
+        column = jnp.sum(jnp.where(lane == my_c * CAP + c, asks, 0.0), axis=1, keepdims=True)
+        hot = jnp.where(place == column.astype(jnp.int32), 1.0, 0.0).astype(bf16)
+        hot_s[c] = hot
+        answers.append(dot(hot, params, ((1,), (1,))))
+    par_x[...] = jnp.concatenate(answers, axis=1).astype(bf16).reshape(par_x.shape)
+
+    copies = exchange(n_c, c_peer, sem_c, 1, lambda o: par_x.at[o], lambda s: par_y.at[my_c])
+    par_y[my_c] = par_x[my_c]
+    finish(copies)
+    block = par_y[...].astype(f32)
+    for z in range(n_z):
+        par_s[z] = block[:, z, :].astype(bf16)
+    copies = exchange(n_z, z_peer, sem_z, 1, lambda o: par_s.at[o], lambda s: par_q.at[my_z])
+    par_q[my_z] = par_s[my_z]
+    finish(copies)
+    turned = par_q[...].astype(f32).reshape(owners, CAP * width).T
+    rows = jnp.zeros((width, n_tiles * slots), f32)
+    for c in range(CAP):
+        rows = rows + dot(
+            turned[c * width : (c + 1) * width].astype(bf16), pick_s[c], ((1,), (0,))
+        )
+    for t in range(n_tiles):
+        rows_s[:, t, :] = rows[:, t * slots : (t + 1) * slots]
+
+    render_tiles(
+        rows_s, ids_ref, pos_ref, cam_ref, cams_ref, target_ref, picture_ref,
+        dx_s, dy_s, exp_s, alpha_s, trans_s, color_s,
+    )
+
+    grads = jnp.concatenate([rows_s[:, t, :] for t in range(n_tiles)], axis=1)
+    parts = pieces(grads)
+    sums = []
+    for c in range(CAP):
+        pick = pick_s[c]
+        sums.append(sum(dot(pick, part, ((1,), (1,))) for part in parts))
+    grad_s[...] = jnp.concatenate(sums, axis=1).reshape(grad_s.shape)
+    copies = exchange(n_z, z_peer, sem_z, 2, lambda o: grad_s.at[o], lambda s: grad_y.at[my_z])
+    grad_y[my_z] = grad_s[my_z]
+    finish(copies)
+    for c in range(n_c):
+        grad_x[c] = grad_y[:, c, :]
+    copies = exchange(n_c, c_peer, sem_c, 2, lambda o: grad_x.at[o], lambda s: grad_u.at[my_c])
+    grad_u[my_c] = grad_x[my_c]
+    finish(copies)
+    turned = grad_u[...].reshape(owners, CAP * width).T
+    total = jnp.zeros((width, g_dev), f32)
+    for c in range(CAP):
+        for part in pieces(turned[c * width : (c + 1) * width]):
+            total = total + dot(part, hot_s[c], ((1,), (0,)))
+
+    chunk = width // n_view
+    local[...] = total.reshape(local.shape)
+    finish(exchange(n_view, v_peer, sem_v, 0, lambda o: local.at[o], lambda s: arrived.at[s - 1]))
+    mine = local[my_view]
+    for step in range(1, n_view):
+        mine = mine + arrived[step - 1]
+    gathered[0] = mine
+    finish(exchange(n_view, v_peer, sem_v, 1, lambda o: gathered.at[0], lambda s: gathered.at[s]))
+    for step in range(n_view):
+        origin = lax.rem(my_view + n_view - step, n_view)
+        out_ref[pl.ds(pl.multiple_of(origin * chunk, chunk), chunk)] = gathered[step]
+
+
+def on_device(params, lists, tile_pos, cam_index, cams, targets):
+    owners = lax.axis_size("gauss")
+    n_view = lax.axis_size("view")
+    n_c = max(2, owners // 16)
+    n_z = owners // n_c
+    width, g_dev = params.shape
     n_tiles, slots = lists.shape
-    lanes = targets.shape[2] // 2
+    half = targets.shape[2] // 2
+    line = CAP * width
+    chunk = width // n_view
+    f32, bf16 = jnp.float32, jnp.bfloat16
     vmem = pl.BlockSpec(memory_space=pltpu.VMEM)
     smem = pl.BlockSpec(memory_space=pltpu.SMEM)
-    plane = pltpu.VMEM((slots, 2 * n_tiles, lanes), jnp.float32)
+    plane = (slots, 2 * n_tiles, half)
+    shapes = [
+        ((n_z, 1, slots), f32),
+        ((n_z, 1, slots), f32),
+        ((n_c, n_z, 1, slots), f32),
+        ((n_c, n_z, line), bf16),
+        ((n_c, n_z, line), bf16),
+        ((n_z, n_c, line), bf16),
+        ((n_z, n_c, line), bf16),
+        ((width, n_tiles, slots), f32),
+        ((n_z, n_c, line), f32),
+        ((n_z, n_c, line), f32),
+        ((n_c, n_z, line), f32),
+        ((n_c, n_z, line), f32),
+        ((CAP, owners, g_dev), bf16),
+        ((CAP, owners, n_tiles * slots), bf16),
+        (plane, f32),
+        (plane, f32),
+        (plane, f32),
+        (plane, f32),
+        (plane, f32),
+        ((3,) + plane, f32),
+        ((n_view, chunk, g_dev), f32),
+        ((n_view - 1, chunk, g_dev), f32),
+        ((n_view, chunk, g_dev), f32),
+    ]
     return pl.pallas_call(
-        render_kernel,
+        lambda *refs: step_kernel(n_view, n_z, n_c, *refs),
         out_shape=(
-            jax.ShapeDtypeStruct(targets.shape, jnp.float32),
-            jax.ShapeDtypeStruct((width, n_tiles, slots), jnp.float32),
+            jax.ShapeDtypeStruct(targets.shape, f32),
+            jax.ShapeDtypeStruct((width, g_dev), f32),
         ),
         in_specs=[vmem, vmem, smem, smem, smem, vmem],
         out_specs=(vmem, vmem),
-        scratch_shapes=[plane] * 5
-        + [pltpu.VMEM((3, slots, 2 * n_tiles, lanes), jnp.float32)],
-        interpret=interpret,
-    )(rows, lists, tile_pos, cam_index, cams, targets)
-
-
-def reduce_kernel(n_view, idx_ref, rows_ref, out_ref, local, arrived, gathered, sem_a, sem_b):
-    me = lax.axis_index("view")
-    width, g_dev = out_ref.shape
-    chunk = width // n_view
-    barrier = pltpu.get_barrier_semaphore()
-    for step in range(1, n_view):
-        pl.semaphore_signal(
-            barrier,
-            inc=1,
-            device_id={"view": lax.rem(me + step, n_view)},
-            device_id_type=pl.DeviceIdType.MESH,
-        )
-    n_idx = idx_ref.shape[1]
-    hot = jnp.where(
-        lax.broadcasted_iota(jnp.int32, (g_dev, n_idx), 0) == idx_ref[...], 1.0, 0.0
-    ).astype(jnp.bfloat16)
-    rest = rows_ref[...]
-    total = jnp.zeros((width, g_dev), jnp.float32)
-    for _ in range(3):
-        piece = rest.astype(jnp.bfloat16)
-        rest = rest - piece.astype(jnp.float32)
-        total = total + lax.dot_general(
-            piece, hot, (((1,), (1,)), ((), ())), preferred_element_type=jnp.float32
-        )
-    local[...] = total.reshape(n_view, chunk, g_dev)
-    pl.semaphore_wait(barrier, n_view - 1)
-    first = []
-    for step in range(1, n_view):
-        peer = lax.rem(me + step, n_view)
-        copy = pltpu.make_async_remote_copy(
-            src_ref=local.at[peer],
-            dst_ref=arrived.at[step - 1],
-            send_sem=sem_a.at[0, step - 1],
-            recv_sem=sem_a.at[1, step - 1],
-            device_id={"view": peer},
-            device_id_type=pl.DeviceIdType.MESH,
-        )
-        copy.start()
-        first.append(copy)
-    for copy in first:
-        copy.wait()
-    mine = local[me]
-    for step in range(1, n_view):
-        mine = mine + arrived[step - 1]
-    gathered[0] = mine
-    second = []
-    for step in range(1, n_view):
-        peer = lax.rem(me + step, n_view)
-        copy = pltpu.make_async_remote_copy(
-            src_ref=gathered.at[0],
-            dst_ref=gathered.at[step],
-            send_sem=sem_b.at[0, step - 1],
-            recv_sem=sem_b.at[1, step - 1],
-            device_id={"view": peer},
-            device_id_type=pl.DeviceIdType.MESH,
-        )
-        copy.start()
-        second.append(copy)
-    for copy in second:
-        copy.wait()
-    for step in range(n_view):
-        origin = lax.rem(me + n_view - step, n_view)
-        out_ref[pl.ds(pl.multiple_of(origin * chunk, chunk), chunk)] = gathered[step]
-
-
-def reduce_call(idx, rows, g_dev):
-    n_view = lax.axis_size("view")
-    width = rows.shape[0]
-    chunk = width // n_view
-    vmem = pl.BlockSpec(memory_space=pltpu.VMEM)
-    return pl.pallas_call(
-        lambda *refs: reduce_kernel(n_view, *refs),
-        out_shape=jax.ShapeDtypeStruct((width, g_dev), jnp.float32),
-        in_specs=[vmem, vmem],
-        out_specs=vmem,
-        scratch_shapes=[
-            pltpu.VMEM((n_view, chunk, g_dev), jnp.float32),
-            pltpu.VMEM((n_view - 1, chunk, g_dev), jnp.float32),
-            pltpu.VMEM((n_view, chunk, g_dev), jnp.float32),
-            pltpu.SemaphoreType.DMA((2, n_view - 1)),
-            pltpu.SemaphoreType.DMA((2, n_view - 1)),
+        scratch_shapes=[pltpu.VMEM(shape, dtype) for shape, dtype in shapes]
+        + [
+            pltpu.SemaphoreType.DMA((3, 2, n_z - 1)),
+            pltpu.SemaphoreType.DMA((3, 2, n_c - 1)),
+            pltpu.SemaphoreType.DMA((2, 2, n_view - 1)),
         ],
         compiler_params=pltpu.CompilerParams(collective_id=0, has_side_effects=True),
-    )(idx, rows)
-
-
-def on_device(params, lists, tile_pos, cam_index, cams, targets):
-    owners = lax.axis_size("gauss")
-    g_dev = params.shape[1]
-    width = params.shape[0]
-    n_tiles, list_len = lists.shape
-    capacity = n_tiles * list_len // owners
-    flat_ids = lists.reshape(-1)
-    is_live = flat_ids >= 0
-    owner_idx = jnp.where(is_live, flat_ids // g_dev, owners)
-    selector = (owner_idx[:, None] == jnp.arange(owners)[None, :]).astype(jnp.int32)
-    ranks = jnp.sum((jnp.cumsum(selector, axis=0) - selector) * selector, axis=1)
-    slot_pos = jnp.where(is_live, owner_idx * capacity + ranks, owners * capacity)
-    read_pos = jnp.minimum(slot_pos, owners * capacity - 1)
-    local_idx = jnp.where(is_live, flat_ids % g_dev, -1)
-    wanted = (
-        jnp.full((owners * capacity,), -1, jnp.int32)
-        .at[slot_pos]
-        .set(local_idx, mode="drop")
-        .reshape(owners, capacity)
-    )
-    received = lax.all_to_all(wanted, "gauss", split_axis=0, concat_axis=0, tiled=True).reshape(-1)
-    picked = jnp.take(params, jnp.maximum(received, 0), axis=1)
-    returned = lax.all_to_all(
-        picked.reshape(width, owners, capacity), "gauss", split_axis=1, concat_axis=1, tiled=True
-    )
-    slot_rows = jnp.take(returned.reshape(width, -1), read_pos, axis=1).reshape(
-        width, n_tiles, list_len
-    )
-    pictures, tile_g = render_call(slot_rows, lists, tile_pos, cam_index, cams, targets)
-    slot_g = tile_g.reshape(width, -1)
-    sent_g = (
-        jnp.zeros((width, owners * capacity), jnp.float32).at[:, slot_pos].set(slot_g, mode="drop")
-    )
-    row_g = lax.all_to_all(
-        sent_g.reshape(width, owners, capacity), "gauss", split_axis=1, concat_axis=1, tiled=True
-    ).reshape(width, -1)
-    grads = reduce_call(received.reshape(1, -1), row_g, g_dev)
-    return (pictures, grads)
+    )(params, lists, tile_pos, cam_index, cams, targets)
 
 
 def solution(mesh):

time: 121 us -> 77 us (0.64)
  Pallas kernels: 23.2 us -> 71.7 us
  waiting for transfers between devices: 43.8 us -> 0 us
  starting transfers between devices: 31.7 us -> 0 us
  local copies, waits for them, and re-layouts: 16.8 us -> 4.36 us
  other arithmetic: 4.22 us -> 0 us
    pallas_call x2 -> x1, Pallas kernels: 23.2 us -> 71.7 us  [on_device(): pl.pallas_call(lambda *refs: step_kernel(n_view, n_z, n_c, *refs), out_sh...]
    all_to_all x3 -> x0, waiting for transfers between devices: 43.8 us -> none  [the longest x1 15.5 us: on_device(): lax.all_to_all(sent_g.reshape(width, owners, capacity), 'gauss', split_ax...]
    all_to_all x3 -> x0, starting transfers between devices: 31.7 us -> none  [the longest x1 20.4 us: on_device(): lax.all_to_all(wanted, 'gauss', split_axis=0, concat_axis=0, tiled=True)]
    scatter x2 -> x0, local copies, waits for them, and re-layouts: 4.21 us -> none  [the longest x1 2.44 us: on_device(): wanted = jnp.full((owners * capacity,), -1, jnp.int32).at[slot_pos].set(l...]
    gather x3 -> x0, local copies, waits for them, and re-layouts: 2.79 us -> none  [the longest x2 1.45 us: on_device(): jnp.take(returned.reshape(width, -1), read_pos, axis=1)]
    all_to_all x2 -> x0, other arithmetic: 1.94 us -> none  [the longest x1 0.99 us: on_device(): lax.all_to_all(wanted, 'gauss', split_axis=0, concat_axis=0, tiled=True)]
    reshape x2 -> x0, local copies, waits for them, and re-layouts: 1.8 us -> none  [the longest x1 1.02 us: on_device(): slot_g = tile_g.reshape(width, -1)]
    all_to_all x3 -> x0, local copies, waits for them, and re-layouts: 1.76 us -> none  [the longest x2 1.25 us: on_device(): lax.all_to_all(wanted, 'gauss', split_axis=0, concat_axis=0, tiled=True)]
  transfers between devices with their start and end apart: 3 -> 0, of which waited for: 3 -> 0; matrix products, arithmetic and copies ran while one was open for 1% -> 0% of each run, Pallas kernels for 0% -> 0%
where the time goes in v2:
time: 77 us; the launch traced here: 76.7 us
  Pallas kernels  71.7 us (93%)
  local copies, waits for them, and re-layouts  4.36 us (6%)
    pallas_call x1, Pallas kernels, on_device(): pl.pallas_call(lambda *refs: step_kernel(n_view, n_z, n_c, *refs), out_sh...  71.7 us
    unnamed x3, local copies, waits for them, and re-layouts  4.36 us

profile of v2, /device:TPU:1, one launch (start us, length us, event | category | flops | bytes accessed | tf_op | source)
XLA Modules:
  0.0 76.7 jit_solution(2992726363079991532)
XLA Ops:
  0.6 1.4 %copy.8.refs_4_ = f32[28,16]{1,0:T(8,128)} copy(f32[28,16]{0,1:T(8,128)} %param.10) | data formatting | bytes 3584 | tf_op args[4]
  2.0 71.7 %shard_map.77 = (f32[3,4,256]{2,1,0:T(4,128)}, f32[64,1024]{1,0:T(8,128)}) custom-call(bf16[64,1024]{1,0:T(8,128)(2,1)} %refs_0_.1, s32[4,128]{1,0:T(4,128)} %refs_1_.1, s32[4]{0:T(128)} %refs_2_.1, s32[4]{0:T(128)} %refs_3_.1, f32[28,16]{1,0:T(8,128)} %copy.8.refs_4_, f32[3,4,256]{2,1,0:T(4,128)} %refs_5_.1), custom_call_target="tpu_custom_call" | custom-call | tf_op jit(solution)/shard_map/pallas_call | solution.py:466
  73.7 1.3 %copy.11 = f32[3,4,256]{2,1,0:T(4,128)} copy(f32[3,4,256]{2,1,0:T(4,128)} %get-tuple-element.4) | data formatting | bytes 24576
  75.0 1.7 %copy.12 = f32[64,1024]{1,0:T(8,128)} copy(f32[64,1024]{1,0:T(8,128)} %get-tuple-element.5) | data formatting | bytes 524288

commit v3 on v2

--- a/solution.py
+++ b/solution.py
@@ -137,26 +137,19 @@
     return out
 
 
+CAP = 4
+ATTRS = 9
+
+
 def render_tiles(
-    rows_ref, ids_ref, pos_ref, cam_ref, cams_ref, target_ref, picture_ref,
+    attr_ref, pos_ref, target_ref, picture_ref,
     dx_s, dy_s, exp_s, alpha_s, trans_s, color_s,
 ):
-    n_tiles, slots = ids_ref.shape
+    n_tiles, slots = attr_ref.shape[1:]
     half = target_ref.shape[2] // 2
     wide = (2 * n_tiles, half)
-    narrow = (n_tiles, slots)
-    live = ids_ref[...] >= 0
-    camcols = [
-        tile_values([cams_ref[row, cam_ref[t]] for t in range(n_tiles)], narrow)
-        for row in range(cams_ref.shape[0])
-    ]
-    row_vals = [rows_ref[row] for row in range(rows_ref.shape[0])]
-    row_vals[6] = jnp.where(live, row_vals[6], 1.0)
-    attrs, pullback = jax.vjp(lambda vals: project(vals, camcols), row_vals)
-    attrs_live = list(attrs)
-    for index in range(9):
-        attrs_live[index] = jnp.where(live, attrs[index], 0.0)
-    attrs8 = [jnp.concatenate([a, a], axis=0) for a in attrs_live]
+    attrs = [attr_ref[row] for row in range(ATTRS)]
+    attrs8 = [jnp.concatenate([a, a], axis=0) for a in attrs]
 
     row_id = lax.broadcasted_iota(jnp.int32, wide, 0)
     lane = lax.broadcasted_iota(jnp.int32, wide, 1)
@@ -228,8 +221,8 @@
 
     _, accs = lax.fori_loop(0, slots // unroll, backward, (zero, (zero,) * 9))
     g0, gx, gy, gxx, gxy, gyy, k0, k1, k2 = [a[:n_tiles] + a[n_tiles:] for a in accs]
-    op = attrs_live[5]
-    ca, cb, cc = attrs_live[2:5]
+    op = attrs[5]
+    ca, cb, cc = attrs[2:5]
     cot = [
         op * (ca * gx + cb * gy),
         op * (cb * gx + cc * gy),
@@ -241,13 +234,8 @@
         k1,
         k2,
     ]
-    cot = [jnp.where(live, value, 0.0) for value in cot]
-    (grads,) = pullback(cot)
-    for row, value in enumerate(grads):
-        rows_ref[row] = jnp.where(live, value, 0.0)
-
-
-CAP = 4
+    for row, value in enumerate(cot):
+        attr_ref[row] = value
 
 
 def pieces(values):
@@ -255,7 +243,12 @@
     for _ in range(3):
         out.append(values.astype(jnp.bfloat16))
         values = values - out[-1].astype(jnp.float32)
-    return out
+    return jnp.concatenate(out, axis=0)
+
+
+def joined(values):
+    third = values.shape[0] // 3
+    return values[:third] + values[third : 2 * third] + values[2 * third :]
 
 
 def dot(a, b, dims):
@@ -266,11 +259,10 @@
     n_view, n_z, n_c,
     params_ref, ids_ref, pos_ref, cam_ref, cams_ref, target_ref,
     picture_ref, out_ref,
-    want_s, ask_a, ask_b, par_x, par_y, par_s, par_q, rows_s,
-    grad_s, grad_y, grad_x, grad_u, hot_s, pick_s,
+    want_s, ask_a, ask_b, par_t, par_x, par_y, par_s, par_q, own_s, cam_s, all_s, all_cam_s,
+    attr_s, grad_s, grad_y, grad_x, grad_u, cot_s, hot_s, pick_s,
     dx_s, dy_s, exp_s, alpha_s, trans_s, color_s,
-    local, arrived, gathered,
-    sem_z, sem_c, sem_v,
+    sem_z, sem_c, sem_g,
 ):
     owners = n_z * n_c
     width, g_dev = params_ref.shape
@@ -284,30 +276,29 @@
         other = lax.rem(my_z + step, n_z)
         return other, {"gauss": other * n_c + my_c}
 
-    def c_peer(step):
-        other = lax.rem(my_c + step, n_c)
-        return other, {"gauss": my_z * n_c + other}
-
-    def v_peer(step):
-        other = lax.rem(my_view + step, n_view)
-        return other, {"view": other}
+    def cv_peer(step):
+        other = lax.rem(my_c + step % n_c, n_c)
+        return other, {
+            "gauss": my_z * n_c + other,
+            "view": lax.rem(my_view + step // n_c, n_view),
+        }
 
     barrier = pltpu.get_barrier_semaphore()
-    for count, peer in ((n_z, z_peer), (n_c, c_peer), (n_view, v_peer)):
+    for count, peer in ((n_z, z_peer), (n_c * n_view, cv_peer)):
         for step in range(1, count):
             pl.semaphore_signal(
                 barrier, inc=1, device_id=peer(step)[1], device_id_type=pl.DeviceIdType.MESH
             )
 
-    def exchange(count, peer, sems, phase, source, target):
+    def exchange(count, peer, sems, source, target):
         copies = []
         for step in range(1, count):
             other, device = peer(step)
             copy = pltpu.make_async_remote_copy(
                 src_ref=source(other),
-                dst_ref=target(step),
-                send_sem=sems.at[phase, 0, step - 1],
-                recv_sem=sems.at[phase, 1, step - 1],
+                dst_ref=target,
+                send_sem=sems.at[0, step - 1],
+                recv_sem=sems.at[1, step - 1],
                 device_id=device,
                 device_id_type=pl.DeviceIdType.MESH,
             )
@@ -320,6 +311,7 @@
             copy.wait()
 
     bits = g_dev.bit_length() - 1
+    base = 2 * g_dev
     own_row = lax.broadcasted_iota(jnp.int32, (owners, slots), 0)
     lane = lax.broadcasted_iota(jnp.int32, (owners, slots), 1)
     before = (
@@ -332,15 +324,15 @@
     for t in range(n_tiles):
         ids = ids_ref[t : t + 1, :]
         owner = lax.shift_right_arithmetic(ids, bits)
-        index = (lax.bitwise_and(ids, g_dev - 1) + 1).astype(f32)
+        code = (lax.bitwise_and(ids, g_dev - 1) + (1 + base * cam_ref[t])).astype(f32)
         named = own_row == owner
         named_f = jnp.where(named, 1.0, 0.0)
         rank = dot(named_f.astype(bf16), before, ((1,), (0,))) + seen
         seen = seen + jnp.sum(named_f, axis=1, keepdims=True)
         for c in range(CAP):
             chosen = jnp.where(rank == float(c), named_f, 0.0)
-            pick_s[c, :, t * slots : (t + 1) * slots] = chosen.astype(bf16)
-            asked[c] = asked[c] + chosen * index
+            pick_s[c * owners : (c + 1) * owners, t * slots : (t + 1) * slots] = chosen.astype(bf16)
+            asked[c] = asked[c] + chosen * code
     spread = jnp.zeros((owners, slots), f32)
     for c in range(CAP):
         column = jnp.sum(asked[c], axis=1, keepdims=True)
@@ -348,80 +340,118 @@
     want = jnp.sum(spread.reshape(n_z, n_c, slots), axis=1)
     for z in range(n_z):
         want_s[z] = want[z : z + 1]
-    pl.semaphore_wait(barrier, n_z + n_c + n_view - 3)
-
-    copies = exchange(n_z, z_peer, sem_z, 0, lambda o: want_s.at[o], lambda s: ask_a.at[my_z])
+    par_t[...] = jnp.zeros(par_t.shape, f32)
+    pl.semaphore_wait(barrier, n_z + n_c * n_view - 2)
+
+    copies = exchange(n_z, z_peer, sem_z.at[0], lambda o: want_s.at[o], ask_a.at[my_z])
     ask_a[my_z] = want_s[my_z]
     finish(copies)
-    copies = exchange(n_c, c_peer, sem_c, 0, lambda o: ask_a, lambda s: ask_b.at[my_c])
-    ask_b[my_c] = ask_a[...]
-    finish(copies)
-    asks = ask_b[...].reshape(owners, slots)
+    asking = exchange(
+        n_c * n_view, cv_peer, sem_g.at[0], lambda o: ask_a, ask_b.at[my_view, my_c]
+    )
+    ask_b[my_view, my_c] = ask_a[...]
+    finish(asking[: n_c - 1])
+
     params = params_ref[...]
-    place = lax.broadcasted_iota(jnp.int32, (owners, g_dev), 1) + 1
-    answers = []
-    for c in range(CAP):
-        column = jnp.sum(jnp.where(lane == my_c * CAP + c, asks, 0.0), axis=1, keepdims=True)
-        hot = jnp.where(place == column.astype(jnp.int32), 1.0, 0.0).astype(bf16)
-        hot_s[c] = hot
-        answers.append(dot(hot, params, ((1,), (1,))))
-    par_x[...] = jnp.concatenate(answers, axis=1).astype(bf16).reshape(par_x.shape)
-
-    copies = exchange(n_c, c_peer, sem_c, 1, lambda o: par_x.at[o], lambda s: par_y.at[my_c])
+    cams3 = pieces(cams_ref[...].T)
+    n_src = n_z * n_c
+    place = lax.broadcasted_iota(jnp.int32, (g_dev, n_src), 0) + 1
+    camera = lax.broadcasted_iota(jnp.int32, (cams_ref.shape[0], n_src), 0)
+    row8 = lax.broadcasted_iota(jnp.int32, (8, slots), 0)
+    lane8 = lax.broadcasted_iota(jnp.int32, (8, slots), 1)
+    mine8 = jnp.where(lane8 == my_c * CAP + row8, 1.0, 0.0).astype(bf16)
+
+    def look_up(asks, rows_ref, cams_out, hot_ref, first):
+        asks = asks.reshape(n_src, slots)
+        codes = jnp.zeros((8, n_src), f32)
+        rest = asks
+        for _ in range(2):
+            part = rest.astype(bf16)
+            rest = rest - part.astype(f32)
+            codes = codes + dot(mine8, part, ((1,), (1,)))
+        codes = codes.astype(jnp.int32)
+        index = lax.bitwise_and(codes, base - 1)
+        seen_by = lax.shift_right_logical(codes, bits + 1)
+        for c in range(CAP):
+            hot = jnp.where(place == index[c : c + 1], 1.0, 0.0).astype(bf16)
+            if hot_ref is not None:
+                hot_ref[:, c * n_src : (c + 1) * n_src] = hot
+            rows_ref[:, first + c, :] = dot(params, hot, ((1,), (0,)))
+            chosen = jnp.where(camera == seen_by[c : c + 1], 1.0, 0.0).astype(bf16)
+            cams_out[:, first + c, :] = joined(dot(cams3, chosen, ((1,), (0,))))
+        return index[:CAP] > 0
+
+    def safe(rows_ref, cams_in, live):
+        row_vals = [rows_ref[row] for row in range(width)]
+        row_vals[6] = jnp.where(live, row_vals[6], 1.0)
+        camcols = [cams_in[row] for row in range(cams_ref.shape[1])]
+        camcols[11] = jnp.where(live, camcols[11], 4.0)
+        return row_vals, camcols
+
+    live = look_up(ask_b[my_view], own_s, cam_s, None, 0)
+    row_vals, camcols = safe(own_s, cam_s, live)
+    for index, value in enumerate(project(row_vals, camcols)):
+        par_t[:CAP, index, :] = value
+    par_x[...] = par_t[...].reshape(8 * 16, n_src).T.reshape(par_x.shape)
+
+    copies = exchange(n_c, cv_peer, sem_c, lambda o: par_x.at[o], par_y.at[my_c])
     par_y[my_c] = par_x[my_c]
     finish(copies)
-    block = par_y[...].astype(f32)
     for z in range(n_z):
-        par_s[z] = block[:, z, :].astype(bf16)
-    copies = exchange(n_z, z_peer, sem_z, 1, lambda o: par_s.at[o], lambda s: par_q.at[my_z])
+        par_s[z] = par_y[:, z, :]
+    copies = exchange(n_z, z_peer, sem_z.at[1], lambda o: par_s.at[o], par_q.at[my_z])
     par_q[my_z] = par_s[my_z]
+
+    finish(asking[n_c - 1 :])
+    lives = [
+        look_up(ask_b[v], all_s, all_cam_s, hot_s.at[v], v * CAP) for v in range(n_view)
+    ]
+    all_live = jnp.concatenate([jnp.where(a, 1.0, 0.0) for a in lives], axis=0) > 0.5
+    row_vals, camcols = safe(all_s, all_cam_s, all_live)
     finish(copies)
-    turned = par_q[...].astype(f32).reshape(owners, CAP * width).T
-    rows = jnp.zeros((width, n_tiles * slots), f32)
-    for c in range(CAP):
-        rows = rows + dot(
-            turned[c * width : (c + 1) * width].astype(bf16), pick_s[c], ((1,), (0,))
-        )
+
+    turned = par_q[...].reshape(owners, 128).T
+    left = jnp.concatenate([pieces(turned[c * 16 : (c + 1) * 16]) for c in range(CAP)], axis=1)
+    found = joined(dot(left, pick_s[...], ((1,), (0,))))
     for t in range(n_tiles):
-        rows_s[:, t, :] = rows[:, t * slots : (t + 1) * slots]
+        attr_s[:, t, :] = found[:, t * slots : (t + 1) * slots]
 
     render_tiles(
-        rows_s, ids_ref, pos_ref, cam_ref, cams_ref, target_ref, picture_ref,
+        attr_s, pos_ref, target_ref, picture_ref,
         dx_s, dy_s, exp_s, alpha_s, trans_s, color_s,
     )
 
-    grads = jnp.concatenate([rows_s[:, t, :] for t in range(n_tiles)], axis=1)
-    parts = pieces(grads)
-    sums = []
-    for c in range(CAP):
-        pick = pick_s[c]
-        sums.append(sum(dot(pick, part, ((1,), (1,))) for part in parts))
-    grad_s[...] = jnp.concatenate(sums, axis=1).reshape(grad_s.shape)
-    copies = exchange(n_z, z_peer, sem_z, 2, lambda o: grad_s.at[o], lambda s: grad_y.at[my_z])
+    grads = jnp.concatenate([attr_s[:, t, :] for t in range(n_tiles)], axis=1)
+    sums = joined(dot(pieces(grads), pick_s[...], ((1,), (1,))))
+    sums = jnp.concatenate(
+        [sums[:, c * owners : (c + 1) * owners] for c in range(CAP)]
+        + [jnp.zeros((128 - 16 * CAP, owners), f32)],
+        axis=0,
+    )
+    grad_s[...] = sums.T.reshape(grad_s.shape)
+    copies = exchange(n_z, z_peer, sem_z.at[2], lambda o: grad_s.at[o], grad_y.at[my_z])
     grad_y[my_z] = grad_s[my_z]
     finish(copies)
     for c in range(n_c):
         grad_x[c] = grad_y[:, c, :]
-    copies = exchange(n_c, c_peer, sem_c, 2, lambda o: grad_x.at[o], lambda s: grad_u.at[my_c])
-    grad_u[my_c] = grad_x[my_c]
+    copies = exchange(
+        n_c * n_view, cv_peer, sem_g.at[1], lambda o: grad_x.at[o], grad_u.at[my_view, my_c]
+    )
+    grad_u[my_view, my_c] = grad_x[my_c]
+    _, pullback = jax.vjp(lambda vals: project(vals, camcols), row_vals)
     finish(copies)
-    turned = grad_u[...].reshape(owners, CAP * width).T
-    total = jnp.zeros((width, g_dev), f32)
-    for c in range(CAP):
-        for part in pieces(turned[c * width : (c + 1) * width]):
-            total = total + dot(part, hot_s[c], ((1,), (0,)))
-
-    chunk = width // n_view
-    local[...] = total.reshape(local.shape)
-    finish(exchange(n_view, v_peer, sem_v, 0, lambda o: local.at[o], lambda s: arrived.at[s - 1]))
-    mine = local[my_view]
-    for step in range(1, n_view):
-        mine = mine + arrived[step - 1]
-    gathered[0] = mine
-    finish(exchange(n_view, v_peer, sem_v, 1, lambda o: gathered.at[0], lambda s: gathered.at[s]))
-    for step in range(n_view):
-        origin = lax.rem(my_view + n_view - step, n_view)
-        out_ref[pl.ds(pl.multiple_of(origin * chunk, chunk), chunk)] = gathered[step]
+    for v in range(n_view):
+        turned = grad_u[v].reshape(n_src, 128).T
+        for c in range(CAP):
+            cot_s[v * CAP + c] = turned[c * 16 : (c + 1) * 16]
+    (grads,) = pullback([cot_s[:, index, :] for index in range(ATTRS)])
+    for row, value in enumerate(grads):
+        all_s[row] = value
+    total = jnp.zeros((3 * width, g_dev), f32)
+    for v in range(n_view):
+        line = jnp.concatenate([all_s[:, v * CAP + c, :] for c in range(CAP)], axis=1)
+        total = total + dot(pieces(line), hot_s[v], ((1,), (1,)))
+    out_ref[...] = joined(total)
 
 
 def on_device(params, lists, tile_pos, cam_index, cams, targets):
@@ -432,8 +462,7 @@
     width, g_dev = params.shape
     n_tiles, slots = lists.shape
     half = targets.shape[2] // 2
-    line = CAP * width
-    chunk = width // n_view
+    rows_c = cams.shape[0]
     f32, bf16 = jnp.float32, jnp.bfloat16
     vmem = pl.BlockSpec(memory_space=pltpu.VMEM)
     smem = pl.BlockSpec(memory_space=pltpu.SMEM)
@@ -441,27 +470,30 @@
     shapes = [
         ((n_z, 1, slots), f32),
         ((n_z, 1, slots), f32),
-        ((n_c, n_z, 1, slots), f32),
-        ((n_c, n_z, line), bf16),
-        ((n_c, n_z, line), bf16),
-        ((n_z, n_c, line), bf16),
-        ((n_z, n_c, line), bf16),
-        ((width, n_tiles, slots), f32),
-        ((n_z, n_c, line), f32),
-        ((n_z, n_c, line), f32),
-        ((n_c, n_z, line), f32),
-        ((n_c, n_z, line), f32),
-        ((CAP, owners, g_dev), bf16),
-        ((CAP, owners, n_tiles * slots), bf16),
+        ((n_view, n_c, n_z, 1, slots), f32),
+        ((8, 16, owners), f32),
+        ((n_c, n_z, 128), f32),
+        ((n_c, n_z, 128), f32),
+        ((n_z, n_c, 128), f32),
+        ((n_z, n_c, 128), f32),
+        ((width, CAP, owners), f32),
+        ((rows_c, CAP, owners), f32),
+        ((width, n_view * CAP, owners), f32),
+        ((rows_c, n_view * CAP, owners), f32),
+        ((16, n_tiles, slots), f32),
+        ((n_z, n_c, 128), f32),
+        ((n_z, n_c, 128), f32),
+        ((n_c, n_z, 128), f32),
+        ((n_view, n_c, n_z, 128), f32),
+        ((n_view * CAP, 16, owners), f32),
+        ((n_view, g_dev, CAP * owners), bf16),
+        ((CAP * owners, n_tiles * slots), bf16),
         (plane, f32),
         (plane, f32),
         (plane, f32),
         (plane, f32),
         (plane, f32),
         ((3,) + plane, f32),
-        ((n_view, chunk, g_dev), f32),
-        ((n_view - 1, chunk, g_dev), f32),
-        ((n_view, chunk, g_dev), f32),
     ]
     return pl.pallas_call(
         lambda *refs: step_kernel(n_view, n_z, n_c, *refs),
@@ -469,16 +501,16 @@
             jax.ShapeDtypeStruct(targets.shape, f32),
             jax.ShapeDtypeStruct((width, g_dev), f32),
         ),
-        in_specs=[vmem, vmem, smem, smem, smem, vmem],
+        in_specs=[vmem, vmem, smem, smem, vmem, vmem],
         out_specs=(vmem, vmem),
         scratch_shapes=[pltpu.VMEM(shape, dtype) for shape, dtype in shapes]
         + [
             pltpu.SemaphoreType.DMA((3, 2, n_z - 1)),
-            pltpu.SemaphoreType.DMA((3, 2, n_c - 1)),
-            pltpu.SemaphoreType.DMA((2, 2, n_view - 1)),
+            pltpu.SemaphoreType.DMA((2, n_c - 1)),
+            pltpu.SemaphoreType.DMA((2, 2, n_c * n_view - 1)),
         ],
         compiler_params=pltpu.CompilerParams(collective_id=0, has_side_effects=True),
-    )(params, lists, tile_pos, cam_index, cams, targets)
+    )(params, lists, tile_pos, cam_index, cams.T, targets)
 
 
 def solution(mesh):

time: 77 us -> 68.6 us (0.89)
  Pallas kernels: 71.7 us -> 64.8 us
  local copies, waits for them, and re-layouts: 4.36 us -> 2.98 us
    pallas_call x1, Pallas kernels: 71.7 us -> 64.8 us  [on_device(): pl.pallas_call(lambda *refs: step_kernel(n_view, n_z, n_c, *refs), out_sh...]
    unnamed x3 -> x2, local copies, waits for them, and re-layouts: 4.36 us -> 2.98 us
where the time goes in v3:
time: 68.6 us; the launch traced here: 68.4 us
  Pallas kernels  64.8 us (94%)
  local copies, waits for them, and re-layouts  2.98 us (4%)
    pallas_call x1, Pallas kernels, on_device(): pl.pallas_call(lambda *refs: step_kernel(n_view, n_z, n_c, *refs), out_sh...  64.8 us
    unnamed x2, local copies, waits for them, and re-layouts  2.98 us

profile of v3, /device:TPU:1, one launch (start us, length us, event | category | flops | bytes accessed | tf_op | source)
XLA Modules:
  0.0 68.4 jit_solution(7561945082046002057)
XLA Ops:
  0.6 64.8 %shard_map.77 = (f32[3,4,256]{2,1,0:T(4,128)}, f32[64,1024]{1,0:T(8,128)}) custom-call(bf16[64,1024]{1,0:T(8,128)(2,1)} %refs_0_.1, s32[4,128]{1,0:T(4,128)} %refs_1_.1, s32[4]{0:T(128)} %refs_2_.1, s32[4]{0:T(128)} %refs_3_.1, f32[16,28]{1,0:T(8,128)} %bitcast.1, f32[3,4,256]{2,1,0:T(4,128)} %refs_5_.1), custom_call_target="tpu_custom_call" | custom-call | tf_op jit(solution)/shard_map/pallas_call | solution.py:498
  65.4 1.3 %copy.10 = f32[3,4,256]{2,1,0:T(4,128)} copy(f32[3,4,256]{2,1,0:T(4,128)} %get-tuple-element.4) | data formatting | bytes 24576
  66.7 1.7 %copy.11 = f32[64,1024]{1,0:T(8,128)} copy(f32[64,1024]{1,0:T(8,128)} %get-tuple-element.5) | data formatting | bytes 524288

commit v4 on v3

--- a/solution.py
+++ b/solution.py
@@ -246,6 +246,24 @@
     return jnp.concatenate(out, axis=0)
 
 
+def two_pieces(values):
+    high = values.astype(jnp.bfloat16)
+    return high, (values - high.astype(jnp.float32)).astype(jnp.bfloat16)
+
+
+def swapped(values):
+    return pltpu.roll(values, 64, axis=1)
+
+
+def folded(values):
+    count = values.shape[0] // 2
+    return values[:count] + swapped(values[count:])
+
+
+def unfolded(values):
+    return jnp.concatenate([values, swapped(values)], axis=0)
+
+
 def joined(values):
     third = values.shape[0] // 3
     return values[:third] + values[third : 2 * third] + values[2 * third :]
@@ -257,9 +275,10 @@
 
 def step_kernel(
     n_view, n_z, n_c,
-    params_ref, ids_ref, pos_ref, cam_ref, cams_ref, target_ref,
+    params_hbm, ids_hbm, pos_hbm, cam_hbm, cams_hbm, target_hbm,
     picture_ref, out_ref,
-    want_s, ask_a, ask_b, par_t, par_x, par_y, par_s, par_q, own_s, cam_s, all_s, all_cam_s,
+    params_ref, ids_ref, pos_ref, cam_ref, cams_ref, target_ref, sem_in,
+    want_s, ask_a, ask_p, ask_b, par_t, par_x, par_y, par_s, par_q, own_s, cam_s, all_s, all_cam_s,
     attr_s, grad_s, grad_y, grad_x, grad_u, cot_s, hot_s, pick_s,
     dx_s, dy_s, exp_s, alpha_s, trans_s, color_s,
     sem_z, sem_c, sem_g,
@@ -289,6 +308,22 @@
             pl.semaphore_signal(
                 barrier, inc=1, device_id=peer(step)[1], device_id_type=pl.DeviceIdType.MESH
             )
+
+    loads = [
+        pltpu.make_async_copy(source, target, sem_in.at[index])
+        for index, (source, target) in enumerate(
+            (
+                (ids_hbm, ids_ref),
+                (cam_hbm, cam_ref),
+                (params_hbm, params_ref),
+                (cams_hbm, cams_ref),
+                (pos_hbm, pos_ref),
+                (target_hbm, target_ref),
+            )
+        )
+    ]
+    for load in loads:
+        load.start()
 
     def exchange(count, peer, sems, source, target):
         copies = []
@@ -312,7 +347,11 @@
 
     bits = g_dev.bit_length() - 1
     base = 2 * g_dev
-    own_row = lax.broadcasted_iota(jnp.int32, (owners, slots), 0)
+    half_c, half_z, n_q = n_c // 2, n_z // 2, n_z // 4
+    row = lax.broadcasted_iota(jnp.int32, (owners, slots), 0)
+    row_z = lax.rem(row // half_c, n_z)
+    row_c = row // (n_z * half_c) * half_c + lax.rem(row, half_c)
+    own_row = row_z * n_c + row_c
     lane = lax.broadcasted_iota(jnp.int32, (owners, slots), 1)
     before = (
         lax.broadcasted_iota(jnp.int32, (slots, slots), 0)
@@ -320,6 +359,8 @@
     )
     before = jnp.where(before, 1.0, 0.0).astype(bf16)
     seen = jnp.zeros((owners, 1), f32)
+    loads[0].wait()
+    loads[1].wait()
     asked = [jnp.zeros((owners, slots), f32) for _ in range(CAP)]
     for t in range(n_tiles):
         ids = ids_ref[t : t + 1, :]
@@ -336,8 +377,15 @@
     spread = jnp.zeros((owners, slots), f32)
     for c in range(CAP):
         column = jnp.sum(asked[c], axis=1, keepdims=True)
-        spread = spread + jnp.where(lane == lax.rem(own_row, n_c) * CAP + c, column, 0.0)
-    want = jnp.sum(spread.reshape(n_z, n_c, slots), axis=1)
+        spread = spread + jnp.where(
+            lane == my_z // n_q * 32 + row_c * CAP + c, column, 0.0
+        )
+    spread = spread[: owners // 2] + spread[owners // 2 :]
+    same = lax.broadcasted_iota(jnp.int32, (n_z, owners // 2), 0) == (
+        lax.broadcasted_iota(jnp.int32, (n_z, owners // 2), 1) // half_c
+    )
+    same = jnp.where(same, 1.0, 0.0).astype(bf16)
+    want = sum(dot(same, part, ((1,), (0,))) for part in two_pieces(spread))
     for z in range(n_z):
         want_s[z] = want[z : z + 1]
     par_t[...] = jnp.zeros(par_t.shape, f32)
@@ -346,29 +394,44 @@
     copies = exchange(n_z, z_peer, sem_z.at[0], lambda o: want_s.at[o], ask_a.at[my_z])
     ask_a[my_z] = want_s[my_z]
     finish(copies)
+    asked = ask_a[...].reshape(n_z, slots)
+    packed = asked[:n_q]
+    for part in range(1, 4):
+        packed = packed + asked[part * n_q : (part + 1) * n_q]
+    ask_p[...] = packed
     asking = exchange(
-        n_c * n_view, cv_peer, sem_g.at[0], lambda o: ask_a, ask_b.at[my_view, my_c]
-    )
-    ask_b[my_view, my_c] = ask_a[...]
+        n_c * n_view, cv_peer, sem_g.at[0], lambda o: ask_p, ask_b.at[my_view, my_c]
+    )
+    ask_b[my_view, my_c] = packed
     finish(asking[: n_c - 1])
 
+    loads[2].wait()
+    loads[3].wait()
     params = params_ref[...]
     cams3 = pieces(cams_ref[...].T)
     n_src = n_z * n_c
     place = lax.broadcasted_iota(jnp.int32, (g_dev, n_src), 0) + 1
     camera = lax.broadcasted_iota(jnp.int32, (cams_ref.shape[0], n_src), 0)
-    row8 = lax.broadcasted_iota(jnp.int32, (8, slots), 0)
-    lane8 = lax.broadcasted_iota(jnp.int32, (8, slots), 1)
-    mine8 = jnp.where(lane8 == my_c * CAP + row8, 1.0, 0.0).astype(bf16)
-
-    def look_up(asks, rows_ref, cams_out, hot_ref, first):
-        asks = asks.reshape(n_src, slots)
+    row32 = lax.broadcasted_iota(jnp.int32, (32, slots), 0)
+    lane32 = lax.broadcasted_iota(jnp.int32, (32, slots), 1)
+    mine32 = lane32 == row32 // 8 * 32 + my_c * CAP + lax.rem(row32, 8)
+    mine32 = jnp.where(mine32, 1.0, 0.0).astype(bf16)
+    line_no = lax.broadcasted_iota(jnp.int32, (n_c * n_q, n_src), 0)
+    src = lax.broadcasted_iota(jnp.int32, (n_c * n_q, n_src), 1)
+    src_z = src // (n_c * half_z) * half_z + lax.rem(src, half_z)
+    src_line = lax.rem(src // half_z, n_c) * n_q + lax.rem(src_z, n_q)
+    orders = [
+        jnp.where((line_no == src_line) & (src_z // n_q == part), 1.0, 0.0).astype(bf16)
+        for part in range(4)
+    ]
+
+    def look_up(view, rows_ref, cams_out, hot_ref, first):
+        lines = jnp.concatenate([ask_b[view, c] for c in range(n_c)], axis=0)
+        found = sum(dot(mine32, part, ((1,), (1,))) for part in two_pieces(lines))
         codes = jnp.zeros((8, n_src), f32)
-        rest = asks
-        for _ in range(2):
-            part = rest.astype(bf16)
-            rest = rest - part.astype(f32)
-            codes = codes + dot(mine8, part, ((1,), (1,)))
+        for index, order in enumerate(orders):
+            for part in two_pieces(found[index * 8 : (index + 1) * 8]):
+                codes = codes + dot(part, order, ((1,), (0,)))
         codes = codes.astype(jnp.int32)
         index = lax.bitwise_and(codes, base - 1)
         seen_by = lax.shift_right_logical(codes, bits + 1)
@@ -388,34 +451,40 @@
         camcols[11] = jnp.where(live, camcols[11], 4.0)
         return row_vals, camcols
 
-    live = look_up(ask_b[my_view], own_s, cam_s, None, 0)
+    live = look_up(my_view, own_s, cam_s, None, 0)
     row_vals, camcols = safe(own_s, cam_s, live)
     for index, value in enumerate(project(row_vals, camcols)):
         par_t[:CAP, index, :] = value
-    par_x[...] = par_t[...].reshape(8 * 16, n_src).T.reshape(par_x.shape)
+    par_x[...] = folded(par_t[...].reshape(8 * 16, n_src).T).reshape(par_x.shape)
 
     copies = exchange(n_c, cv_peer, sem_c, lambda o: par_x.at[o], par_y.at[my_c])
     par_y[my_c] = par_x[my_c]
     finish(copies)
-    for z in range(n_z):
-        par_s[z] = par_y[:, z, :]
+    low_c = lax.broadcasted_iota(jnp.int32, (half_c, 128), 1) < 64
+    for z in range(half_z):
+        lines = par_y[:, z, :]
+        other = swapped(lines)
+        par_s[z] = jnp.where(low_c, lines[:half_c], other[half_c:])
+        par_s[half_z + z] = jnp.where(low_c, other[:half_c], lines[half_c:])
     copies = exchange(n_z, z_peer, sem_z.at[1], lambda o: par_s.at[o], par_q.at[my_z])
     par_q[my_z] = par_s[my_z]
 
     finish(asking[n_c - 1 :])
     lives = [
-        look_up(ask_b[v], all_s, all_cam_s, hot_s.at[v], v * CAP) for v in range(n_view)
+        look_up(v, all_s, all_cam_s, hot_s.at[v], v * CAP) for v in range(n_view)
     ]
     all_live = jnp.concatenate([jnp.where(a, 1.0, 0.0) for a in lives], axis=0) > 0.5
     row_vals, camcols = safe(all_s, all_cam_s, all_live)
     finish(copies)
 
-    turned = par_q[...].reshape(owners, 128).T
+    turned = unfolded(par_q[...].reshape(owners // 2, 128)).T
     left = jnp.concatenate([pieces(turned[c * 16 : (c + 1) * 16]) for c in range(CAP)], axis=1)
     found = joined(dot(left, pick_s[...], ((1,), (0,))))
     for t in range(n_tiles):
         attr_s[:, t, :] = found[:, t * slots : (t + 1) * slots]
 
+    loads[4].wait()
+    loads[5].wait()
     render_tiles(
         attr_s, pos_ref, target_ref, picture_ref,
         dx_s, dy_s, exp_s, alpha_s, trans_s, color_s,
@@ -428,12 +497,16 @@
         + [jnp.zeros((128 - 16 * CAP, owners), f32)],
         axis=0,
     )
-    grad_s[...] = sums.T.reshape(grad_s.shape)
+    grad_s[...] = folded(sums.T).reshape(grad_s.shape)
     copies = exchange(n_z, z_peer, sem_z.at[2], lambda o: grad_s.at[o], grad_y.at[my_z])
     grad_y[my_z] = grad_s[my_z]
     finish(copies)
-    for c in range(n_c):
-        grad_x[c] = grad_y[:, c, :]
+    low_z = lax.broadcasted_iota(jnp.int32, (half_z, 128), 1) < 64
+    for c in range(half_c):
+        lines = grad_y[:, c, :]
+        other = swapped(lines)
+        grad_x[c] = jnp.where(low_z, lines[:half_z], other[half_z:])
+        grad_x[half_c + c] = jnp.where(low_z, other[:half_z], lines[half_z:])
     copies = exchange(
         n_c * n_view, cv_peer, sem_g.at[1], lambda o: grad_x.at[o], grad_u.at[my_view, my_c]
     )
@@ -441,7 +514,7 @@
     _, pullback = jax.vjp(lambda vals: project(vals, camcols), row_vals)
     finish(copies)
     for v in range(n_view):
-        turned = grad_u[v].reshape(n_src, 128).T
+        turned = unfolded(grad_u[v].reshape(n_src // 2, 128)).T
         for c in range(CAP):
             cot_s[v * CAP + c] = turned[c * 16 : (c + 1) * 16]
     (grads,) = pullback([cot_s[:, index, :] for index in range(ATTRS)])
@@ -465,26 +538,26 @@
     rows_c = cams.shape[0]
     f32, bf16 = jnp.float32, jnp.bfloat16
     vmem = pl.BlockSpec(memory_space=pltpu.VMEM)
-    smem = pl.BlockSpec(memory_space=pltpu.SMEM)
     plane = (slots, 2 * n_tiles, half)
     shapes = [
         ((n_z, 1, slots), f32),
         ((n_z, 1, slots), f32),
-        ((n_view, n_c, n_z, 1, slots), f32),
+        ((n_z // 4, slots), f32),
+        ((n_view, n_c, n_z // 4, slots), f32),
         ((8, 16, owners), f32),
-        ((n_c, n_z, 128), f32),
-        ((n_c, n_z, 128), f32),
-        ((n_z, n_c, 128), f32),
-        ((n_z, n_c, 128), f32),
+        ((n_c, n_z // 2, 128), f32),
+        ((n_c, n_z // 2, 128), f32),
+        ((n_z, n_c // 2, 128), f32),
+        ((n_z, n_c // 2, 128), f32),
         ((width, CAP, owners), f32),
         ((rows_c, CAP, owners), f32),
         ((width, n_view * CAP, owners), f32),
         ((rows_c, n_view * CAP, owners), f32),
         ((16, n_tiles, slots), f32),
-        ((n_z, n_c, 128), f32),
-        ((n_z, n_c, 128), f32),
-        ((n_c, n_z, 128), f32),
-        ((n_view, n_c, n_z, 128), f32),
+        ((n_z, n_c // 2, 128), f32),
+        ((n_z, n_c // 2, 128), f32),
+        ((n_c, n_z // 2, 128), f32),
+        ((n_view, n_c, n_z // 2, 128), f32),
         ((n_view * CAP, 16, owners), f32),
         ((n_view, g_dev, CAP * owners), bf16),
         ((CAP * owners, n_tiles * slots), bf16),
@@ -501,9 +574,18 @@
             jax.ShapeDtypeStruct(targets.shape, f32),
             jax.ShapeDtypeStruct((width, g_dev), f32),
         ),
-        in_specs=[vmem, vmem, smem, smem, vmem, vmem],
+        in_specs=[pl.BlockSpec(memory_space=pl.ANY)] * 6,
         out_specs=(vmem, vmem),
-        scratch_shapes=[pltpu.VMEM(shape, dtype) for shape, dtype in shapes]
+        scratch_shapes=[
+            pltpu.VMEM(params.shape, params.dtype),
+            pltpu.VMEM(lists.shape, lists.dtype),
+            pltpu.SMEM(tile_pos.shape, tile_pos.dtype),
+            pltpu.SMEM(cam_index.shape, cam_index.dtype),
+            pltpu.VMEM(cams.shape[::-1], cams.dtype),
+            pltpu.VMEM(targets.shape, targets.dtype),
+            pltpu.SemaphoreType.DMA((6,)),
+        ]
+        + [pltpu.VMEM(shape, dtype) for shape, dtype in shapes]
         + [
             pltpu.SemaphoreType.DMA((3, 2, n_z - 1)),
             pltpu.SemaphoreType.DMA((2, n_c - 1)),

time: 68.6 us -> 65.5 us (0.955)
  Pallas kernels: 64.8 us -> 61.7 us
    pallas_call x1, Pallas kernels: 64.8 us -> 61.7 us  [on_device(): pl.pallas_call(lambda *refs: step_kernel(n_view, n_z, n_c, *refs), out_sh...]
where the time goes in v4:
time: 65.5 us; the launch traced here: 65.3 us
  Pallas kernels  61.7 us (94%)
  local copies, waits for them, and re-layouts  2.98 us (5%)
    pallas_call x1, Pallas kernels, on_device(): pl.pallas_call(lambda *refs: step_kernel(n_view, n_z, n_c, *refs), out_sh...  61.7 us
    unnamed x2, local copies, waits for them, and re-layouts  2.98 us

profile of v4, /device:TPU:1, one launch (start us, length us, event | category | flops | bytes accessed | tf_op | source)
XLA Modules:
  0.0 65.3 jit_solution(575895517309811919)
XLA Ops:
  0.6 61.7 %shard_map.77 = (f32[3,4,256]{2,1,0:T(4,128)}, f32[64,1024]{1,0:T(8,128)}) custom-call(bf16[64,1024]{1,0:T(8,128)(2,1)} %refs_0_.1, s32[4,128]{1,0:T(4,128)} %refs_1_.1, s32[4]{0:T(128)} %refs_2_.1, s32[4]{0:T(128)} %refs_3_.1, f32[16,28]{1,0:T(8,128)} %bitcast.1, f32[3,4,256]{2,1,0:T(4,128)} %refs_5_.1), custom_call_target="tpu_custom_call" | custom-call | tf_op jit(solution)/shard_map/pallas_call | solution.py:571
  62.3 1.3 %copy.10 = f32[3,4,256]{2,1,0:T(4,128)} copy(f32[3,4,256]{2,1,0:T(4,128)} %get-tuple-element.4) | data formatting | bytes 24576
  63.7 1.7 %copy.11 = f32[64,1024]{1,0:T(8,128)} copy(f32[64,1024]{1,0:T(8,128)} %get-tuple-element.5) | data formatting | bytes 524288

commit v5 on v4

--- a/solution.py
+++ b/solution.py
@@ -163,7 +163,7 @@
         at = jnp.full(wide, slot, jnp.int32)
         return jnp.take_along_axis(values, at, axis=1, mode="promise_in_bounds")
 
-    unroll = 8
+    unroll = 16
 
     def forward(step, carry):
         trans, r0, r1, r2 = carry
@@ -571,8 +571,8 @@
     return pl.pallas_call(
         lambda *refs: step_kernel(n_view, n_z, n_c, *refs),
         out_shape=(
-            jax.ShapeDtypeStruct(targets.shape, f32),
-            jax.ShapeDtypeStruct((width, g_dev), f32),
+            pltpu.VMEM(targets.shape, f32),
+            pltpu.VMEM((width, g_dev), f32),
         ),
         in_specs=[pl.BlockSpec(memory_space=pl.ANY)] * 6,
         out_specs=(vmem, vmem),

time: 65.5 us -> 61.8 us (0.944)
  Pallas kernels: 61.7 us -> 59.7 us
  local copies, waits for them, and re-layouts: 2.98 us -> 1.3 us
    pallas_call x1, Pallas kernels: 61.7 us -> 59.7 us  [on_device(): pl.pallas_call(lambda *refs: step_kernel(n_view, n_z, n_c, *refs), out_sh...]
    unnamed x2, local copies, waits for them, and re-layouts: 2.98 us -> 1.3 us
where the time goes in v5:
time: 61.8 us; the launch traced here: 61.6 us
  Pallas kernels  59.7 us (97%)
  local copies, waits for them, and re-layouts  1.3 us (2%)
  between operations  0.64 us (1%)
    pallas_call x1, Pallas kernels, on_device(): pl.pallas_call(lambda *refs: step_kernel(n_view, n_z, n_c, *refs), out_sh...  59.7 us
    unnamed x2, local copies, waits for them, and re-layouts  1.3 us

profile of v5, /device:TPU:1, one launch (start us, length us, event | category | flops | bytes accessed | tf_op | source)
XLA Modules:
  0.0 61.6 jit_solution(6183897810100207113)
XLA Ops:
  0.6 59.7 %shard_map.77 = (f32[3,4,256]{2,1,0:T(4,128)S(1)}, f32[64,1024]{1,0:T(8,128)S(1)}) custom-call(bf16[64,1024]{1,0:T(8,128)(2,1)} %refs_0_.1, s32[4,128]{1,0:T(4,128)} %refs_1_.1, s32[4]{0:T(128)} %refs_2_.1, s32[4]{0:T(128)} %refs_3_.1, f32[16,28]{1,0:T(8,128)} %bitcast.1, f32[3,4,256]{2,1,0:T(4,128)} %refs_5_.1), custom_call_target="tpu_custom_call" | custom-call | tf_op jit(solution)/shard_map/pallas_call | solution.py:571
  60.3 0.6 copy.10
  60.9 0.7 %copy.11 = f32[64,1024]{1,0:T(8,128)} copy(f32[64,1024]{1,0:T(8,128)S(1)} %get-tuple-element.3) | data formatting | bytes 524288

commit v6 on v5

--- a/solution.py
+++ b/solution.py
@@ -291,6 +291,9 @@
     my_view = lax.axis_index("view")
     my_z, my_c = me // n_c, lax.rem(me, n_c)
 
+    def far_first(count):
+        return sorted(range(1, count), key=lambda step: -min(step, count - step))
+
     def z_peer(step):
         other = lax.rem(my_z + step, n_z)
         return other, {"gauss": other * n_c + my_c}
@@ -304,7 +307,7 @@
 
     barrier = pltpu.get_barrier_semaphore()
     for count, peer in ((n_z, z_peer), (n_c * n_view, cv_peer)):
-        for step in range(1, count):
+        for step in far_first(count):
             pl.semaphore_signal(
                 barrier, inc=1, device_id=peer(step)[1], device_id_type=pl.DeviceIdType.MESH
             )
@@ -337,8 +340,9 @@
                 device_id=device,
                 device_id_type=pl.DeviceIdType.MESH,
             )
-            copy.start()
             copies.append(copy)
+        for step in far_first(count) if count == n_z else range(1, count):
+            copies[step - 1].start()
         return copies
 
     def finish(copies):
@@ -512,8 +516,9 @@
     )
     grad_u[my_view, my_c] = grad_x[my_c]
     _, pullback = jax.vjp(lambda vals: project(vals, camcols), row_vals)
-    finish(copies)
-    for v in range(n_view):
+    for step in sorted(range(n_view), key=lambda step: min(step, n_view - step)):
+        finish(copies[max(step * n_c - 1, 0) : (step + 1) * n_c - 1])
+        v = lax.rem(my_view + n_view - step, n_view)
         turned = unfolded(grad_u[v].reshape(n_src // 2, 128)).T
         for c in range(CAP):
             cot_s[v * CAP + c] = turned[c * 16 : (c + 1) * 16]

time: 61.8 us -> 61.6 us (level)
  no operation moved by 1% of the time
where the time goes in v6:
time: 61.6 us; the launch traced here: 61.5 us
  Pallas kernels  59.5 us (97%)
  local copies, waits for them, and re-layouts  1.3 us (2%)
  between operations  0.64 us (1%)
    pallas_call x1, Pallas kernels, on_device(): pl.pallas_call(lambda *refs: step_kernel(n_view, n_z, n_c, *refs), out_sh...  59.5 us
    unnamed x2, local copies, waits for them, and re-layouts  1.3 us

profile of v6, /device:TPU:1, one launch (start us, length us, event | category | flops | bytes accessed | tf_op | source)
XLA Modules:
  0.0 61.5 jit_solution(9018747708873021896)
XLA Ops:
  0.6 59.5 %shard_map.77 = (f32[3,4,256]{2,1,0:T(4,128)S(1)}, f32[64,1024]{1,0:T(8,128)S(1)}) custom-call(bf16[64,1024]{1,0:T(8,128)(2,1)} %refs_0_.1, s32[4,128]{1,0:T(4,128)} %refs_1_.1, s32[4]{0:T(128)} %refs_2_.1, s32[4]{0:T(128)} %refs_3_.1, f32[16,28]{1,0:T(8,128)} %bitcast.1, f32[3,4,256]{2,1,0:T(4,128)} %refs_5_.1), custom_call_target="tpu_custom_call" | custom-call | tf_op jit(solution)/shard_map/pallas_call | solution.py:576
  60.2 0.6 copy.10
  60.8 0.7 %copy.11 = f32[64,1024]{1,0:T(8,128)} copy(f32[64,1024]{1,0:T(8,128)S(1)} %get-tuple-element.3) | data formatting | bytes 524288

commit v7 on v5

--- a/solution.py
+++ b/solution.py
@@ -163,7 +163,7 @@
         at = jnp.full(wide, slot, jnp.int32)
         return jnp.take_along_axis(values, at, axis=1, mode="promise_in_bounds")
 
-    unroll = 16
+    unroll = 32
 
     def forward(step, carry):
         trans, r0, r1, r2 = carry

time: 61.8 us -> 61.1 us (0.989)
  Pallas kernels: 59.7 us -> 59 us
    pallas_call x1, Pallas kernels: 59.7 us -> 59 us  [on_device(): pl.pallas_call(lambda *refs: step_kernel(n_view, n_z, n_c, *refs), out_sh...]
where the time goes in v7:
time: 61.1 us; the launch traced here: 61 us
  Pallas kernels  59 us (97%)
  local copies, waits for them, and re-layouts  1.3 us (2%)
  between operations  0.64 us (1%)
    pallas_call x1, Pallas kernels, on_device(): pl.pallas_call(lambda *refs: step_kernel(n_view, n_z, n_c, *refs), out_sh...  59 us
    unnamed x2, local copies, waits for them, and re-layouts  1.3 us

profile of v7, /device:TPU:1, one launch (start us, length us, event | category | flops | bytes accessed | tf_op | source)
XLA Modules:
  0.0 61.0 jit_solution(10318948699783184585)
XLA Ops:
  0.6 59.0 %shard_map.77 = (f32[3,4,256]{2,1,0:T(4,128)S(1)}, f32[64,1024]{1,0:T(8,128)S(1)}) custom-call(bf16[64,1024]{1,0:T(8,128)(2,1)} %refs_0_.1, s32[4,128]{1,0:T(4,128)} %refs_1_.1, s32[4]{0:T(128)} %refs_2_.1, s32[4]{0:T(128)} %refs_3_.1, f32[16,28]{1,0:T(8,128)} %bitcast.1, f32[3,4,256]{2,1,0:T(4,128)} %refs_5_.1), custom_call_target="tpu_custom_call" | custom-call | tf_op jit(solution)/shard_map/pallas_call | solution.py:571
  59.7 0.6 copy.10
  60.3 0.7 %copy.11 = f32[64,1024]{1,0:T(8,128)} copy(f32[64,1024]{1,0:T(8,128)S(1)} %get-tuple-element.3) | data formatting | bytes 524288
